TPU v7x, 512 devices: a whole 4x8x8 slice. The times are simulated.
512 devices in a mesh: grow: 16 (over y, core), gcol: 32 (over x, z).
Axes of the slice: x: 4, y: 8, z: 8, core: 2. Of those that a mesh axis runs over, the one named last changes fastest.
Arguments:
- pair_density: bfloat16 [16384, 2048], P('gcol', 'grow'), may hold values from -0.125 to 0.125
- pair_weight: float32 [2048], P('grow'), may hold values from 0.25 to 4
- coulomb: float32 [16384], replicated, may hold values from 0.25 to 4
- pivot_rows: int32 [512], replicated, may hold values from 0 to 16383, as said below
Outputs:
- dielectric: float32 [16384, 16384], P('grow', 'gcol')
- panel_factor: float32 [16384, 512], P('grow')
Inputs may be any that keep to these rules, and one draw needn't show every extreme that they name: `pivot_rows`: 512 distinct plane-wave indices, exactly one in each run of 32 consecutive plane waves starting at a multiple of it; 0 and 16383 are always among them.
All inputs are finite; a program needn't handle non-finite values.
Results may differ from a plain program's by a relative error of at most 0.0038.
Values may be sent and summed in bfloat16 or wider, within the bound.
A program may use at most 64 MiB of HBM per device.

v0:
```python
import jax
import jax.numpy as jnp
from jax import lax
from jax.sharding import Mesh
from jax.sharding import PartitionSpec as P

NG = 16384
PANEL = 512
GCOL = ("gcol_0", "gcol_1")
GROW = ("grow_0", "grow_1")


def joined_along(blocks, dim):
    lengths = list(blocks.shape[1:])
    lengths[dim] *= blocks.shape[0]
    return jnp.moveaxis(blocks, 0, dim).reshape(lengths)


def gather_in_order(x, axes, sequence):
    blocks = x
    for k in sequence:
        blocks = lax.all_gather(blocks, axes[k])
    done = sequence[::-1]
    back = [done.index(k) for k in range(len(axes))]
    blocks = blocks.transpose(*back, *range(len(axes), blocks.ndim))
    return blocks.reshape(-1, *x.shape)


def gather_axes(x, axes, sequence, dim):
    return joined_along(gather_in_order(x, axes, sequence), dim)


def sent_to_all(x, axis):
    length = lax.axis_size(axis)
    return lax.all_to_all(jnp.broadcast_to(x[None], (length, *x.shape)), axis, 0, 0, tiled=True)


def collect(x, axis, dim):
    return joined_along(sent_to_all(x, axis), dim)


def padded_to(lines, length):
    spare = -len(lines) % length
    return jnp.pad(lines, [(0, spare)] + [(0, 0)] * (lines.ndim - 1))


def reduced_to_own(blocks, axes, sequence):
    lengths = [lax.axis_size(a) for a in axes]
    blocks = blocks.reshape(*lengths, *blocks.shape[1:])
    blocks = blocks.transpose(*sequence, *range(len(axes), blocks.ndim))
    blocks = blocks.reshape(-1, *blocks.shape[len(axes) :])
    for k in sequence:
        blocks = lax.psum_scatter(blocks, axes[k], scatter_dimension=0, tiled=True)
    return blocks[0]


def sum_by_parts(x, axes, sequence):
    length, lines = (lax.axis_size(axes), x.reshape(-1, *x.shape[1:][-1:]))
    blocks = padded_to(lines, length).reshape(length, -1, *lines.shape[1:])
    own = reduced_to_own(blocks, axes, sequence)
    whole = gather_in_order(own, axes, sequence[::-1]).reshape(-1, *lines.shape[1:])
    return whole[: len(lines)].reshape(x.shape)


def factor_rows(columns_in, row_numbers, pivot_block, pivot_rows):
    width = pivot_rows.shape[0]
    factor = jnp.linalg.cholesky(pivot_block)
    pivot_diag = jnp.diagonal(factor)
    solved = lax.linalg.triangular_solve(
        factor, columns_in, left_side=False, lower=True, transpose_a=True
    )
    lower_part = solved / pivot_diag[None, :]
    upper = pivot_diag[:, None] * factor.T
    column_iota = lax.iota(jnp.int32, width)
    matches = row_numbers[:, None] == pivot_rows[None, :]
    is_pivot = jnp.any(matches, axis=1)
    position = jnp.sum(jnp.where(matches, column_iota[None, :], 0), axis=1)
    top_rows = jnp.take(upper, position, axis=0)
    upper_mask = is_pivot[:, None] & (column_iota[None, :] >= position[:, None])
    return jnp.where(upper_mask, top_rows, lower_part)


def select_rows(columns_in, first_row, pivot_rows):
    count_rows = columns_in.shape[0]
    offsets = pivot_rows - first_row
    inside = (offsets >= 0) & (offsets < count_rows)
    taken = jnp.take(columns_in, jnp.clip(offsets, 0, count_rows - 1), axis=0)
    return jnp.where(inside[:, None], taken, 0.0)


def body(pair_density, pair_weight, coulomb, pivot_rows):
    col_ratio = lax.axis_size(GCOL) // lax.axis_size(GROW)
    row_id = lax.axis_index(GROW)
    col_id = lax.axis_index(GCOL)
    scaled = (pair_density.astype(jnp.float32) * jnp.sqrt(pair_weight)[None, :]).astype(
        jnp.bfloat16
    )
    width_cols = scaled.shape[0]
    width_rows = width_cols * col_ratio
    contract = (((1,), (1,)), ((), ()))
    every_wave = gather_axes(scaled, GCOL, (0, 1), 0)
    row_side = lax.all_to_all(every_wave, GROW, split_axis=0, concat_axis=1, tiled=True)
    gram_block = lax.dot_general(
        row_side, collect(scaled, GROW, 1), contract, preferred_element_type=jnp.float32
    )
    first_global = row_id * width_rows
    row_numbers = first_global + lax.iota(jnp.int32, width_rows)
    col_numbers = col_id * width_cols + lax.iota(jnp.int32, width_cols)
    row_scale = jnp.sqrt(lax.dynamic_slice_in_dim(coulomb, first_global, width_rows))
    col_scale = jnp.sqrt(lax.dynamic_slice_in_dim(coulomb, col_id * width_cols, width_cols))
    identity = jnp.where(row_numbers[:, None] == col_numbers[None, :], 1.0, 0.0).astype(jnp.float32)
    dielectric = row_scale[:, None] * col_scale[None, :] * gram_block + identity
    stride = NG // PANEL
    per_device = width_cols // stride
    run_of = pivot_rows // stride
    run_pivot = jnp.zeros((PANEL,), jnp.int32).at[run_of].set(pivot_rows)
    local_cols = (
        lax.dynamic_slice_in_dim(run_pivot, col_id * per_device, per_device) - col_id * width_cols
    )
    own_columns = jnp.take(dielectric, local_cols, axis=1)
    run_columns = lax.all_gather(own_columns, GCOL, axis=1, tiled=True)
    columns = jnp.take(run_columns, run_of, axis=1)
    pivot_block = sum_by_parts(select_rows(columns, first_global, pivot_rows), GROW, (0, 1))
    panel_out = factor_rows(columns, row_numbers, pivot_block, pivot_rows)
    return (dielectric, panel_out)


def solution(mesh):
    finer = Mesh(mesh.devices.reshape(8, 2, 4, 8), ("grow_0", "grow_1", "gcol_0", "gcol_1"))
    return jax.shard_map(
        body,
        mesh=finer,
        in_specs=(P(GCOL, GROW), P(GROW), P(), P()),
        out_specs=(P(GROW, GCOL), P(GROW, None)),
        check_vma=False,
    )
```

profile of v0, /device:TPU:1, one launch (start us, length us, event | category | flops | bytes accessed | tf_op | source)
XLA Modules:
  0.0 577.8 jit_solution(7937591395494677095)
XLA Ops:
  7.2 0.7 sqrt.11
  7.9 0.9 multiply_convert_fusion
  8.8 12.2 %all-gather = bf16[2048,128]{1,0:T(8,128)(2,1)} all-gather(bf16[512,128]{1,0:T(8,128)(2,1)S(1)} %multiply_convert_fusion), channel_id=2, replica_groups=mesh['grow_0'=8,'grow_1'=2,'gcol_0'=4,'gcol_1'=8] {'gcol_0'}, dimensions={0}, use_global_device_ids=true | all-gather | bytes 655360 | tf_op jit(solution)/shard_map/all_gather | solution.py:22
  21.1 1.7 broadcast_in_dim.109
  22.8 11.8 %all-to-all-start.1 = ((bf16[16,512,128]{2,1,0:T(8,128)(2,1)}), bf16[16,512,128]{2,1,0:T(8,128)(2,1)S(1)}, u32[]{:S(2)}, u32[]{:S(2)}) async-start(bf16[16,512,128]{2,1,0:T(8,128)(2,1)} %broadcast_in_dim.109), calls=%async_computation.1 | async-start | bytes 4194304 | tf_op jit(solution)/shard_map/all_to_all | solution.py:35
  34.6 51.9 %all-gather.9.cloned.1.call-done = bf16[32,512,128]{2,1,0:T(8,128)(2,1)} async-done(((bf16[4,512,128]{2,1,0:T(8,128)(2,1)}), bf16[32,512,128]{2,1,0:T(8,128)(2,1)}) %all-gather.9.cloned.1.call-update) | async-done | bytes 4194320 | tf_op jit(solution)/shard_map/all_gather | solution.py:22
  86.4 4.6 copy.20
  91.0 7.7 %all-to-all-start = ((bf16[16,1024,128]{2,1,0:T(8,128)(2,1)}), bf16[16,1024,128]{2,1,0:T(8,128)(2,1)}, u32[]{:S(2)}, u32[]{:S(2)}) async-start(bf16[16,1024,128]{2,1,0:T(8,128)(2,1)} %bitcast.81), calls=%async_computation | async-start | bytes 8388608 | tf_op jit(solution)/shard_map/all_to_all | solution.py:102
  98.8 2.4 scatter_custom_fusion
  101.4 0.8 dynamic-slice_sqrt_fusion.1
  102.1 0.7 dynamic-slice_sqrt_fusion
  102.8 89.4 %all-to-all-done = bf16[16,1024,128]{2,1,0:T(8,128)(2,1)} async-done(((bf16[16,1024,128]{2,1,0:T(8,128)(2,1)}), bf16[16,1024,128]{2,1,0:T(8,128)(2,1)}, u32[]{:S(2)}, u32[]{:S(2)}) %all-to-all-start) | async-done | bytes 4194336 | tf_op jit(solution)/shard_map/all_to_all | solution.py:102
  192.2 5.9 %fusion.4 = f32[1024,512]{1,0:T(8,128)} fusion(bf16[16,512,128]{2,1,0:T(8,128)(2,1)S(1)} %all-to-all-done.1, bf16[16,1024,128]{2,1,0:T(8,128)(2,1)} %all-to-all-done, s32[512]{0:T(512)S(1)} %iota_add_fusion.1, f32[512]{0:T(512)S(1)} %dynamic-slice_sqrt_fusion.1, f32[1024]{0:T(1024)S(1)} %dynamic-slice_sqrt_fusion, s32[1024]{0:T(1024)S(1)} %iota_add_fusion), kind=kOutput, calls=%fused_computation.16 | convolution fusion | flops 2150105088 | bytes 8400896 | tf_op jit(solution)/shard_map/dot_general | solution.py:103
  198.2 1.9 copy.21
  200.7 0.7 select_bitcast_fusion.1
  201.7 75.1 %all-gather.7.cloned.1.call-done = f32[1024,512]{0,1:T(8,128)} async-done(((f32[1024,16]{0,1:T(8,128)}), f32[1024,512]{0,1:T(8,128)}) %all-gather.7.cloned.1.call-update) | async-done | bytes 2097168 | tf_op jit(solution)/shard_map/all_gather | solution.py:121
  276.8 4.4 gather_fusion.1
  281.2 1.8 copy.22
  283.0 1.8 select_bitcast_fusion
  284.9 1.6 gather_fusion.2
  286.5 1.2 select_select_fusion.1
  287.7 38.0 %reduce-scatter.3.cloned.1.call-done = f32[2,32,512]{2,1,0:T(8,128)} async-done(((f32[16,32,512]{2,1,0:T(8,128)}), f32[2,32,512]{2,1,0:T(8,128)}) %reduce-scatter.3.cloned.1.call-update) | async-done | bytes 131088 | tf_op jit(solution)/shard_map/reduce_scatter | solution.py:53
  325.8 23.9 %reduce-scatter.5.cloned.1.call-done = f32[1,32,512]{2,1,0:T(8,128)} async-done(((f32[2,32,512]{2,1,0:T(8,128)}), f32[1,32,512]{2,1,0:T(8,128)}) %reduce-scatter.5.cloned.1.call-update) | async-done | bytes 65552 | tf_op jit(solution)/shard_map/reduce_scatter | solution.py:53
  349.7 3.8 all_gather.29
  354.5 35.1 %all-gather.11.cloned.1.call-done = f32[16,32,512]{2,1,0:T(8,128)} async-done(((f32[2,32,512]{2,1,0:T(8,128)}), f32[16,32,512]{2,1,0:T(8,128)}) %all-gather.11.cloned.1.call-update) | async-done | bytes 1048592 | tf_op jit(solution)/shard_map/all_gather | solution.py:22
  389.6 2.6 copy.23
  392.2 1.4 fusion.23
  393.6 1.0 copy-done.8
  394.6 11.7 %cholesky.102 = f32[128,128]{1,0:T(8,128)S(1)} custom-call(f32[128,128]{1,0:T(8,128)S(1)} %cholesky.260), custom_call_target="Cholesky" | custom-call | tf_op jit(solution)/shard_map/jit(cholesky)/cholesky | solution.py:67
  406.3 9.8 %custom-call.30 = f32[1,128,128]{1,2,0:T(8,128)S(1)} custom-call(f32[1,128,128]{2,1,0:T(8,128)S(1)} %get-tuple-element.43), custom_call_target="InvertDiagBlocksLowerTriangular" | custom-call | tf_op jit(solution)/shard_map/jit(cholesky)/cholesky | solution.py:67
  416.3 1.2 constant_dynamic-update-slice_fusion.3
  417.5 1.3 convolution_subtract_fusion.2
  418.8 11.7 %cholesky.213 = f32[128,128]{1,0:T(8,128)S(1)} custom-call(f32[128,128]{1,0:T(8,128)S(1)} %cholesky.264), custom_call_target="Cholesky" | custom-call | tf_op jit(solution)/shard_map/jit(cholesky)/cholesky | solution.py:67
  430.6 9.9 %custom-call.31 = f32[1,128,128]{1,2,0:T(8,128)S(1)} custom-call(f32[1,128,128]{2,1,0:T(8,128)S(1)} %get-tuple-element.40), custom_call_target="InvertDiagBlocksLowerTriangular" | custom-call | tf_op jit(solution)/shard_map/jit(cholesky)/cholesky | solution.py:67
  440.8 1.3 convolution_subtract_fusion.3
  442.1 11.7 %cholesky.234 = f32[128,128]{1,0:T(8,128)S(1)} custom-call(f32[128,128]{1,0:T(8,128)S(1)} %cholesky.269), custom_call_target="Cholesky" | custom-call | tf_op jit(solution)/shard_map/jit(cholesky)/cholesky | solution.py:67
  453.8 0.7 compare_reduce_fusion.2
  454.5 9.8 %custom-call.32 = f32[1,128,128]{1,2,0:T(8,128)S(1)} custom-call(f32[1,128,128]{2,1,0:T(8,128)S(1)} %get-tuple-element.37), custom_call_target="InvertDiagBlocksLowerTriangular" | custom-call | tf_op jit(solution)/shard_map/jit(cholesky)/cholesky | solution.py:67
  464.6 1.2 convolution_subtract_fusion.4
  465.8 11.9 %cholesky.251 = f32[128,128]{1,0:T(8,128)S(1)} custom-call(f32[128,128]{1,0:T(8,128)S(1)} %convolution_subtract_fusion.4), custom_call_target="Cholesky" | custom-call | tf_op jit(solution)/shard_map/jit(cholesky)/cholesky | solution.py:67
  477.8 0.8 compare_reduce_fusion.1
  478.6 0.6 compare_reduce_fusion.3
  481.6 2.4 fusion.24
  484.0 4.5 gather_fusion.3
  488.5 1.1 multiply_bitcast_fusion
  489.6 1.6 copy.24
  491.2 14.0 %while.1 = (s32[]{:T(128)}, f32[512,512]{1,0:T(8,128)}, s32[4,2]{0,1:T(2,128)S(1)}, f32[4,128,128]{2,1,0:T(8,128)}, s32[]{:T(128)}) while((s32[]{:T(128)}, f32[512,512]{1,0:T(8,128)}, s32[4,2]{0,1:T(2,128)S(1)}, f32[4,128,128]{2,1,0:T(8,128)}, s32[]{:T(128)}) %tuple.42), condition=%wide.while_cond, body=%wide.while_body.sunk | while | flops 2 | bytes 132205 | solution.py:69
  491.3 0.6 fusion.57
  491.9 2.9 bitcast_dynamic-update-slice_fusion.2
  495.4 2.9 bitcast_dynamic-update-slice_fusion.2
  498.9 2.9 bitcast_dynamic-update-slice_fusion.2
  502.4 2.8 bitcast_dynamic-update-slice_fusion.2
  505.2 40.1 %custom-call.33 = f32[4,128,128]{1,2,0:T(8,128)S(1)} custom-call(f32[4,128,128]{2,1,0:T(8,128)} %get-tuple-element.9), custom_call_target="InvertDiagBlocksLowerTriangular" | custom-call | tf_op jit(solution)/shard_map/triangular_solve | solution.py:69
  545.4 0.6 fusion.25
  546.0 1.9 convolution_subtract_fusion.1
  547.9 0.6 fusion.37
  548.5 2.9 convolution_subtract_fusion
  551.4 0.6 fusion.36
  552.0 3.8 fusion.17
  555.9 0.6 fusion.35
  556.5 4.9 gather_fusion.4
  561.4 3.0 copy.25
  564.4 3.7 fusion.3
  568.1 2.9 copy.26
  (66 shorter events, 4.9 us)
Async XLA Ops:
  7.2 79.3 %all-gather.9.cloned.1.call-start = ((), (), s32[]{:S(2)}) async-start(), calls=%async_computation.7 | async-start | bytes 4718592 | tf_op jit(solution)/shard_map/all_gather | solution.py:22
  22.8 68.2 %all-to-all-start.1 = ((bf16[16,512,128]{2,1,0:T(8,128)(2,1)}), bf16[16,512,128]{2,1,0:T(8,128)(2,1)S(1)}, u32[]{:S(2)}, u32[]{:S(2)}) async-start(bf16[16,512,128]{2,1,0:T(8,128)(2,1)} %broadcast_in_dim.109), calls=%async_computation.1 | async-start | bytes 4194304 | tf_op jit(solution)/shard_map/all_to_all | solution.py:35
  91.0 7.8 %copy-start.9 = (s32[512]{0:T(512)S(1)}, s32[512]{0:T(512)}, u32[]{:S(2)}) copy-start(s32[512]{0:T(512)} %param.7) | copy-start | bytes 6148
  91.0 101.2 %all-to-all-start = ((bf16[16,1024,128]{2,1,0:T(8,128)(2,1)}), bf16[16,1024,128]{2,1,0:T(8,128)(2,1)}, u32[]{:S(2)}, u32[]{:S(2)}) async-start(bf16[16,1024,128]{2,1,0:T(8,128)(2,1)} %bitcast.81), calls=%async_computation | async-start | bytes 8388608 | tf_op jit(solution)/shard_map/all_to_all | solution.py:102
  98.7 178.1 %all-gather.7.cloned.1.call-start = ((), (), s32[]{:S(2)}) async-start(), calls=%async_computation.4 | async-start | bytes 2162688 | tf_op jit(solution)/shard_map/all_gather | solution.py:121
  201.4 124.3 %reduce-scatter.3.cloned.1.call-start = ((), (), s32[]{:S(2)}) async-start(), calls=%async_computation.5 | async-start | bytes 1179648 | tf_op jit(solution)/shard_map/reduce_scatter | solution.py:53
  287.7 62.0 %reduce-scatter.5.cloned.1.call-start = ((), (), s32[]{:S(2)}) async-start(), calls=%async_computation.6 | async-start | bytes 196608 | tf_op jit(solution)/shard_map/reduce_scatter | solution.py:53
  325.8 63.9 %all-gather.11.cloned.1.call-start = ((), (), s32[]{:S(2)}) async-start(), calls=%async_computation.8 | async-start | bytes 1179648 | tf_op jit(solution)/shard_map/all_gather | solution.py:22
  389.6 2.6 copy-start.7
  393.6 1.0 copy-start.8
  477.7 3.9 copy-start.4
  546.0 6.1 %copy-start = (f32[1024,128]{0,1:T(8,128)}, f32[1024,128]{0,1:T(8,128)S(1)}, u32[]{:S(2)}) copy-start(f32[1024,128]{0,1:T(8,128)S(1)} %fusion.25) | copy-start | bytes 1572868
  548.5 7.3 %copy-start.2 = (f32[1024,128]{0,1:T(8,128)}, f32[1024,128]{0,1:T(8,128)S(1)}, u32[]{:S(2)}) copy-start(f32[1024,128]{0,1:T(8,128)S(1)} %fusion.37) | copy-start | bytes 1572868
  552.0 3.8 copy-start.5
  561.4 3.1 copy-start.1
  561.4 3.1 copy-start.3
  561.4 3.1 copy-start.6
Sparse Core Ops, SparseCore 0:
  21.2 65.2 all-gather.8
  201.5 75.2 all-gather.6
  287.8 37.8 reduce-scatter.2
  328.3 21.2 reduce-scatter.4
  353.6 35.9 all-gather.10
where the time goes:
time: 588 us; the launch traced here: 578 us
  waiting for transfers between devices  314 us (53%)
  other arithmetic  133 us (23%)
  local copies, waits for them, and re-layouts  56 us (10%)
  matrix products  22.4 us (4%)
  starting transfers between devices  19.7 us (3%)
  between operations  16.8 us (3%)
  blocking collectives  16 us (3%)
    all_to_all x1, waiting for transfers between devices, body(): lax.all_to_all(every_wave, GROW, split_axis=0, concat_axis=1, tiled=True)  89.4 us
    all_gather x2, waiting for transfers between devices, gather_in_order(): blocks = lax.all_gather(blocks, axes[k])  87 us
    another operation x14, other arithmetic, factor_rows(): factor = jnp.linalg.cholesky(pivot_block)  78.9 us
    all_gather x1, waiting for transfers between devices, body(): run_columns = lax.all_gather(own_columns, GCOL, axis=1, tiled=True)  75.1 us
    reduce_scatter x2, waiting for transfers between devices, reduced_to_own(): blocks = lax.psum_scatter(blocks, axes[k], scatter_dimension=0, tiled=True)  61.9 us
    another operation x3, other arithmetic, factor_rows(): lax.linalg.triangular_solve(factor, columns_in, left_side=False, lower=Tr...  42.5 us
    all_gather x2, blocking collectives, gather_in_order(): blocks = lax.all_gather(blocks, axes[k])  16 us
    another operation x12, local copies, waits for them, and re-layouts  14 us
  transfers between devices with their start and end apart: 7, of which 6 were waited for; matrix products, arithmetic and copies ran while one was open for 2% of the time, Pallas kernels for 0%

commit v1 on v0

v1 whole, which is shorter than its diff:
```python
import functools

import jax
import jax.numpy as jnp
from jax import lax
from jax.experimental import pallas as pl
from jax.experimental.pallas import tpu as pltpu
from jax.sharding import Mesh
from jax.sharding import PartitionSpec as P

NG = 16384
PANEL = 512
RUN = NG // PANEL
NY, NC, NX, NZ = 8, 2, 4, 8
COLS = NG // (NX * NZ)
ROWS = NG // (NY * NC)
OWN = 128
HALF = NY * OWN
MINE = COLS // RUN
HI = lax.Precision.HIGHEST
f32, bf16 = jnp.float32, jnp.bfloat16
MESH_ID = pl.DeviceIdType.MESH


def iota(shape, dim):
    return lax.broadcasted_iota(jnp.int32, shape, dim)


def eye(n):
    return iota((n, n), 0) == iota((n, n), 1)


def column_of(row):
    blocks = []
    for i in range(row.shape[1] // 128):
        part = jnp.broadcast_to(row[:, i * 128 : (i + 1) * 128], (128, 128))
        blocks.append(jnp.sum(jnp.where(eye(128), part, 0.0), axis=1, keepdims=True))
    return jnp.concatenate(blocks, axis=0)


def row_of(column):
    blocks = []
    for i in range(column.shape[0] // 128):
        part = jnp.broadcast_to(column[i * 128 : (i + 1) * 128], (128, 128))
        blocks.append(jnp.sum(jnp.where(eye(128), part, 0.0), axis=0, keepdims=True))
    return jnp.concatenate(blocks, axis=1)


def lanes_of(ref, first, count):
    return jnp.concatenate([ref[pl.ds(first + i, 1), :] for i in range(count)], axis=1)


def times_t(a, b, precision=None):
    return lax.dot_general(
        a, b, (((1,), (1,)), ((), ())), precision=precision, preferred_element_type=f32
    )


def t_times(a, b, precision=None):
    return lax.dot_general(
        a, b, (((0,), (0,)), ((), ())), precision=precision, preferred_element_type=f32
    )


def split3(y):
    high = y.astype(bf16).astype(f32)
    rest = y - high
    middle = rest.astype(bf16).astype(f32)
    return high, middle, rest - middle


def eight_rows(s_ref, c):
    sub = iota((8, 128), 0)
    rows = s_ref[c : c + 8, :]
    cols = [jnp.broadcast_to(rows[:, c + j : c + j + 1], (8, 128)) for j in range(8)]
    left, right = rows[:, :128], rows[:, 128:]
    for j in range(8):
        r = lax.rsqrt(jnp.broadcast_to(cols[j][j : j + 1, :], (8, 128)))
        f = jnp.where(sub > j, cols[j] * r, 0.0)
        own = jnp.where(sub == j, r, 1.0)
        for m in range(j + 1, 8):
            cols[m] = cols[m] - f * (jnp.broadcast_to(cols[m][j : j + 1, :], (8, 128)) * r)
        left_j = jnp.broadcast_to(left[j : j + 1, :], (8, 128)) * r
        right_j = jnp.broadcast_to(right[j : j + 1, :], (8, 128)) * r
        left = left * own - f * left_j
        right = right * own - f * right_j
    y = jnp.concatenate([left, right], axis=1)
    s_ref[c : c + 8, :] = y
    if c + 8 < 128:
        h, m, l = split3(y)
        lhs = jnp.concatenate([h, h, m, h, l, m], axis=0)[:, :128].astype(bf16)
        rhs = jnp.concatenate([h, m, h, l, h, m], axis=0).astype(bf16)
        s_ref[c + 8 :, :] = s_ref[c + 8 :, :] - t_times(lhs, rhs)[c + 8 :, :]


def factor_and_inverse(aug, s_ref, between):
    def block(k, carry):
        o = pl.multiple_of(k * 128, 128)
        s_ref[:, :128] = aug[pl.ds(o, 128), pl.ds(o, 128)]
        s_ref[:, 128:] = eye(128).astype(f32)
        for b in range(16):
            eight_rows(s_ref, 8 * b)
            between(k, b)
        aug[pl.ds(o, 128), :] = jnp.dot(
            s_ref[:, 128:], aug[pl.ds(o, 128), :], precision=HI, preferred_element_type=f32
        )
        for i in range(1, 4):

            @pl.when(i > k)
            def _():
                lhs = aug[pl.ds(o, 128), i * 128 : (i + 1) * 128]
                update = t_times(lhs, aug[pl.ds(o, 128), :], HI)
                aug[i * 128 : (i + 1) * 128, :] = aug[i * 128 : (i + 1) * 128, :] - update

        return carry

    lax.fori_loop(0, 4, block, 0)


def prologue(density_ref, weight_ref, pivots_ref, scaled_ref, picked_ref):
    first = (lax.axis_index("x") * NZ + lax.axis_index("z")) * COLS
    scaled = (density_ref[...].astype(f32) * jnp.sqrt(weight_ref[...])).astype(bf16)
    scaled_ref[...] = scaled
    pivots = column_of(jnp.concatenate([pivots_ref[i : i + 1, :] for i in range(4)], axis=1).astype(f32))
    waves = (first + iota((PANEL, COLS), 1)).astype(f32)
    taken = jnp.sum(jnp.where(pivots == waves, 1.0, 0.0), axis=0, keepdims=True)
    in_run = iota((MINE, COLS), 1) // RUN == iota((MINE, COLS), 0)
    one_hot = jnp.where(in_run, jnp.broadcast_to(taken, (MINE, COLS)), 0.0).astype(bf16)
    picked_ref[...] = jnp.dot(one_hot, scaled, preferred_element_type=f32).astype(bf16)


class Gather:
    def __init__(self, slot, line, sems, place):
        self.slot, self.line, self.sems, self.place = slot, line, sems, place

    def ring_z(self, view, step, base):
        y, c, x, z = self.place
        send, recv = self.sems
        out = []
        right, left = lax.rem(z + 1, NZ), lax.rem(z + NZ - 1, NZ)
        from_left = lax.rem(z + NZ - step + 1, NZ), lax.rem(z + NZ - step, NZ)
        k = base + 2 * (step - 1)
        out.append((view(from_left[0]), view(from_left[1]), k, (y, c, x, right)))
        if step < 4:
            from_right = lax.rem(z + step - 1, NZ), lax.rem(z + step, NZ)
            out.append((view(from_right[0]), view(from_right[1]), k + 1, (y, c, x, left)))
        return out

    def ring_x(self, view, half, step, base):
        y, c, x, z = self.place
        right, left = lax.rem(x + 1, NX), lax.rem(x + NX - 1, NX)
        opposite = lax.rem(x + 2, NX)
        k = base + 2 * (step - 1)
        if step == 1:
            return [
                (view(x), view(left), k, (y, c, right, z)),
                (view(x), view(right), k + 1, (y, c, left, z)),
            ]
        return [
            (half(left, 0), half(opposite, 0), k, (y, c, right, z)),
            (half(right, 1), half(opposite, 1), k + 1, (y, c, left, z)),
        ]

    def copies(self, core, step):
        x, z = self.place[2], self.place[3]
        if core == 0:
            if step < 4:
                return self.ring_z(lambda i: self.slot(x, i), step + 1, 0)
            return self.ring_x(
                lambda i: self.line(0, i), lambda i, h: self.line(0, i, h), step - 3, 7
            )
        if step < 2:
            return self.ring_x(
                lambda i: self.slot(i, z), lambda i, h: self.slot(i, z, h), step + 1, 7
            )
        return self.ring_z(lambda i: self.line(1, i), step - 1, 0)

    def each(self, core, step, do):
        send, recv = self.sems
        for sent, received, k, device in self.copies(core, step):
            do(sent, received, send.at[k], recv.at[k], device)

    def start(self, core, step):
        def go(sent, received, s, r, device):
            pltpu.make_async_remote_copy(sent, sent, s, r, device, MESH_ID).start()

        self.each(core, step, go)

    def wait_recv(self, core, step):
        def go(sent, received, s, r, device):
            pltpu.make_async_remote_copy(received, received, s, r, device, MESH_ID).wait_recv()

        self.each(core, step, go)

    def wait_send(self, core, step):
        def go(sent, received, s, r, device):
            pltpu.make_async_remote_copy(sent, sent, s, r, device, MESH_ID).wait_send()

        self.each(core, step, go)

    def advance(self, event):
        for core in range(2):

            @pl.when(self.place[1] == core)
            def _():
                if event > 0:
                    self.wait_recv(core, event - 1)
                if event < 6:
                    self.start(core, event)

    def drain(self):
        for core in range(2):

            @pl.when(self.place[1] == core)
            def _():
                for step in range(6):
                    self.wait_send(core, step)


def main_kernel(
    scaled_ref,
    picked_ref,
    coulomb_ref,
    pivots_ref,
    dielectric_ref,
    panel_ref,
    q_ref,
    r_ref,
    c_ref,
    qp_ref,
    aug,
    s_ref,
    columns_ref,
    local_sem,
    qy_send,
    qy_recv,
    qg_send,
    qg_recv,
    rg_send,
    rg_recv,
    cy_send,
    cy_recv,
    one_send,
    one_recv,
):
    y, c, x, z = (lax.axis_index(a) for a in ("y", "c", "x", "z"))
    place = (y, c, x, z)
    partner = (y, 1 - c, x, z)

    def shift(plane, core):
        return lax.rem(plane + 12 - 4 * lax.rem(plane, 2) - 2 * core, NY)

    to_y, to_c = 2 * x + z // 4, lax.rem(z // 2, 2)
    to_half = lax.rem(z, 2)
    target = (to_y, to_c, 2 * to_half + c, lax.rem(y + NZ - shift(to_y, to_c), NZ))
    mine = shift(y, c)

    def owner_of(zz):
        return lax.rem(zz + mine, NY)

    origin = (owner_of(z), lax.rem(x, 2), y // 2, 4 * lax.rem(y, 2) + 2 * c + x // 2)

    def r_block(pair_core, half, owner):
        return r_ref.at[
            pair_core,
            pl.ds(pl.multiple_of(half * COLS, COLS), COLS),
            pl.ds(pl.multiple_of(owner * OWN, OWN), OWN),
        ]

    def r_slot(xx, zz, part=None):
        first, count = (xx // 2) * COLS, COLS
        if part is not None:
            first, count = first + part * (COLS // 2), COLS // 2
        return r_ref.at[
            lax.rem(xx, 2),
            pl.ds(pl.multiple_of(first, 256), count),
            pl.ds(pl.multiple_of(owner_of(zz) * OWN, OWN), OWN),
        ]

    def r_line(core, i, part=None):
        if core == 0:
            first, count = (i // 2) * COLS, COLS
            if part is not None:
                first, count = first + part * (COLS // 2), COLS // 2
            return r_ref.at[lax.rem(i, 2), pl.ds(pl.multiple_of(first, 256), count), :]
        return r_ref.at[:, :, pl.ds(pl.multiple_of(owner_of(i) * OWN, OWN), OWN)]

    def q_slot(xx, zz, part=None):
        rows = pl.ds(pl.multiple_of(zz * MINE, MINE), MINE)
        cols = slice(None) if part is None else pl.ds(part * (HALF // 2), HALF // 2)
        return q_ref.at[c, xx, rows, cols]

    def q_line(core, i, part=None):
        if core == 0:
            rows = slice(None) if part is None else pl.ds(part * 64, 64)
            return q_ref.at[c, i, rows, :]
        return q_ref.at[c, :, pl.ds(pl.multiple_of(i * MINE, MINE), MINE), :]

    q_gather = Gather(q_slot, q_line, (qg_send, qg_recv), place)
    r_gather = Gather(r_slot, r_line, (rg_send, rg_recv), place)

    barrier = pltpu.get_barrier_semaphore()
    greeted = [(lax.rem(y + d, NY), c, x, z) for d in range(1, NY)]
    greeted += [(y, c, x, lax.rem(z + d, NZ)) for d in (1, NZ - 1)]
    greeted += [(y, c, lax.rem(x + d, NX), z) for d in (1, NX - 1)]
    greeted += [partner, target, origin]
    for device in greeted:
        pl.semaphore_signal(barrier, 1, device_id=device, device_id_type=MESH_ID)

    own_q = q_ref.at[c, x, pl.ds(pl.multiple_of(z * MINE, MINE), MINE), pl.ds(pl.multiple_of(y * OWN, OWN), OWN)]
    own_c = c_ref.at[c, :, pl.ds(pl.multiple_of(y * OWN, OWN), OWN)]
    keep_q = pltpu.make_async_copy(picked_ref, own_q, local_sem.at[0])
    keep_c = pltpu.make_async_copy(scaled_ref, own_c, local_sem.at[1])
    keep_q.start()
    keep_c.start()
    pl.semaphore_wait(barrier, len(greeted))

    def picked_copy(d):
        peer = (lax.rem(y + d, NY), c, x, z)
        return pltpu.make_async_remote_copy(
            picked_ref, own_q, qy_send.at[d], qy_recv.at[d], peer, MESH_ID
        )

    def picked_arrival(d):
        other = lax.rem(y + NY - d, NY)
        there = q_ref.at[c, x, pl.ds(pl.multiple_of(z * MINE, MINE), MINE), pl.ds(pl.multiple_of(other * OWN, OWN), OWN)]
        return pltpu.make_async_remote_copy(
            there, there, qy_send.at[d], qy_recv.at[d], partner, MESH_ID
        )

    for d in (4, 3, 5, 2, 6, 1, 7):
        picked_copy(d).start()

    spread = pltpu.make_async_remote_copy(
        scaled_ref, r_block(c, to_half, y), one_send.at[0], one_recv.at[0], target, MESH_ID
    )
    arrived = r_slot(x, z)
    spread_in = pltpu.make_async_remote_copy(
        arrived, arrived, one_send.at[0], one_recv.at[0], origin, MESH_ID
    )

    def c_of(owner):
        return c_ref.at[c, :, pl.ds(pl.multiple_of(owner * OWN, OWN), OWN)]

    def ring_y(step):
        up, down = (lax.rem(y + 1, NY), c, x, z), (lax.rem(y + NY - 1, NY), c, x, z)
        k = 2 * (step - 1)
        out = [(c_of(lax.rem(y + NY - step + 1, NY)), c_of(lax.rem(y + NY - step, NY)), k, up)]
        if step < 4:
            out.append((c_of(lax.rem(y + step - 1, NY)), c_of(lax.rem(y + step, NY)), k + 1, down))
        return out

    def c_copies(step, received):
        for sent, came, k, device in ring_y(step):
            ref = came if received else sent
            yield pltpu.make_async_remote_copy(ref, ref, cy_send.at[k], cy_recv.at[k], device, MESH_ID)

    def half_of(ref, k):
        ours, theirs = ref.at[c], ref.at[1 - c]
        out = pltpu.make_async_remote_copy(ours, ours, one_send.at[k], one_recv.at[k], partner, MESH_ID)
        back = pltpu.make_async_remote_copy(theirs, theirs, one_send.at[k], one_recv.at[k], partner, MESH_ID)
        return out, back

    q_out, q_back = half_of(q_ref, 1)
    c_out, c_back = half_of(c_ref, 2)

    def c_advance(event):
        if event > 1:
            for copy in c_copies(event - 1, True):
                copy.wait_recv()
        if event < 5:
            for copy in c_copies(event, False):
                copy.start()
        if event == 5:
            c_out.start()

    keep_q.wait()
    for d in range(1, NY):
        picked_arrival(d).wait_recv()
    q_gather.advance(0)
    spread.start()
    keep_c.wait()
    c_advance(1)

    pivot_row = jnp.concatenate([pivots_ref[i : i + 1, :] for i in range(4)], axis=1)
    run_column = column_of((pivot_row // RUN).astype(f32))
    high_column = column_of((pivot_row // 128).astype(f32))
    low_column = column_of((pivot_row % 128).astype(f32))
    in_row = (high_column == iota((PANEL, 128), 1).astype(f32)).astype(f32)
    picked = jnp.dot(in_row, coulomb_ref[...], precision=HI, preferred_element_type=f32)
    at_lane = low_column == iota((PANEL, 128), 1).astype(f32)
    pivot_scale = jnp.sqrt(jnp.sum(jnp.where(at_lane, picked, 0.0), axis=1, keepdims=True))
    pivot_scale_row = row_of(pivot_scale)
    order = (run_column == iota((PANEL, PANEL), 1).astype(f32)).astype(bf16)

    for event in range(1, 7):
        q_gather.advance(event)
        if event == 3:
            c_advance(2)
    q_out.start()
    q_back.wait_recv()

    gram = None
    for h in range(2):
        qp_ref[h] = jnp.dot(
            order, q_ref[h].reshape(PANEL, HALF), preferred_element_type=f32
        ).astype(bf16)
        part = times_t(qp_ref[h], qp_ref[h])
        gram = part if gram is None else gram + part
    unit = eye(PANEL).astype(f32)
    aug[:, :PANEL] = pivot_scale * pivot_scale_row * gram + unit
    aug[:, PANEL:] = unit

    def between(k, b):
        def at(block, event):
            @pl.when(k == block)
            def _():
                event()

        if b == 0:

            @pl.when(k == 0)
            def _():
                spread_in.wait_recv()

            at(0, lambda: r_gather.advance(0))
            at(1, lambda: r_gather.advance(2))
            at(2, lambda: r_gather.advance(4))
            at(0, lambda: c_advance(3))
            at(1, lambda: c_advance(5))
        if b == 8:
            at(0, lambda: r_gather.advance(1))
            at(1, lambda: r_gather.advance(3))
            at(2, lambda: r_gather.advance(5))
            at(0, lambda: c_advance(4))

    factor_and_inverse(aug, s_ref, between)

    lt = aug[:, :PANEL]
    row_i, col_i = iota((PANEL, PANEL), 0), iota((PANEL, PANEL), 1)
    diag = jnp.sum(jnp.where(row_i == col_i, lt, 0.0), axis=1, keepdims=True)
    upper = jnp.where(col_i >= row_i, lt * diag, 0.0)
    aug[:, PANEL:] = aug[:, PANEL:] / diag

    c_back.wait_recv()
    r_gather.advance(6)

    first_row = (y * NC + c) * ROWS
    first_col = (x * NZ + z) * COLS
    row_scale = jnp.sqrt(column_of(lanes_of(coulomb_ref, (y * NC + c) * 8, 8)))
    col_scale = jnp.sqrt(lanes_of(coulomb_ref, (x * NZ + z) * 4, 4))
    tile = 256
    for t in range(ROWS // tile):
        rows = slice(t * tile, (t + 1) * tile)
        scale = row_scale[rows]
        numbers = first_row + t * tile + iota((tile, COLS), 0)
        gram = times_t(r_ref[0, rows, :], c_ref[0]) + times_t(r_ref[1, rows, :], c_ref[1])
        same = numbers == first_col + iota((tile, COLS), 1)
        dielectric_ref[rows, :] = scale * col_scale * gram + jnp.where(same, 1.0, 0.0)
        gram = times_t(r_ref[0, rows, :], qp_ref[0]) + times_t(r_ref[1, rows, :], qp_ref[1])
        same = numbers == pivot_row
        columns_ref[...] = scale * pivot_scale_row * gram + jnp.where(same, 1.0, 0.0)
        panel_ref[rows, :256] = times_t(columns_ref[:, :256], aug[:256, PANEL : PANEL + 256], HI)
        panel_ref[rows, 256:] = times_t(columns_ref[...], aug[256:, PANEL:], HI)

    runs = ROWS // RUN
    run_row = pivot_row // RUN
    mine_here = run_row == (y * NC + c) * runs + iota((runs, PANEL), 0)
    pick = mine_here.astype(f32)
    top = jnp.dot(pick, upper, precision=HI, preferred_element_type=f32)
    position = jnp.sum(pick * iota((runs, PANEL), 1).astype(f32), axis=1, keepdims=True)
    within = jnp.sum(pick * jnp.broadcast_to((pivot_row % RUN).astype(f32), (runs, PANEL)), axis=1, keepdims=True)
    lane = iota((RUN, PANEL), 1).astype(f32)
    line = iota((RUN, PANEL), 0).astype(f32)
    for q in range(runs):
        rows = slice(q * RUN, (q + 1) * RUN)
        over = (line == within[q : q + 1]) & (lane >= position[q : q + 1])
        panel_ref[rows, :] = jnp.where(over, jnp.broadcast_to(top[q : q + 1, :], (RUN, PANEL)), panel_ref[rows, :])

    for d in range(1, NY):
        picked_copy(d).wait_send()
    spread.wait_send()
    for step in range(1, 5):
        for copy in c_copies(step, False):
            copy.wait_send()
    q_out.wait_send()
    c_out.wait_send()
    q_gather.drain()
    r_gather.drain()


def body(pair_density, pair_weight, coulomb, pivot_rows):
    vmem = pl.BlockSpec(memory_space=pltpu.VMEM)
    pivots = pivot_rows.reshape(4, 128)
    scaled, picked = pl.pallas_call(
        prologue,
        out_shape=(
            jax.ShapeDtypeStruct((COLS, OWN), bf16),
            jax.ShapeDtypeStruct((MINE, OWN), bf16),
        ),
        in_specs=[vmem] * 3,
        out_specs=(vmem, vmem),
        name="scale_and_pick",
    )(pair_density, pair_weight.reshape(1, OWN), pivots)
    dma = pltpu.SemaphoreType.DMA
    return pl.pallas_call(
        main_kernel,
        out_shape=(
            jax.ShapeDtypeStruct((ROWS, COLS), f32),
            jax.ShapeDtypeStruct((ROWS, PANEL), f32),
        ),
        in_specs=[vmem] * 4,
        out_specs=(vmem, vmem),
        scratch_shapes=[
            pltpu.VMEM((2, NX, NZ * MINE, HALF), bf16),
            pltpu.VMEM((2, ROWS, HALF), bf16),
            pltpu.VMEM((2, COLS, HALF), bf16),
            pltpu.VMEM((2, PANEL, HALF), bf16),
            pltpu.VMEM((PANEL, 2 * PANEL), f32),
            pltpu.VMEM((128, 256), f32),
            pltpu.VMEM((256, PANEL), f32),
            dma((2,)),
            dma((NY,)),
            dma((NY,)),
            dma((11,)),
            dma((11,)),
            dma((11,)),
            dma((11,)),
            dma((7,)),
            dma((7,)),
            dma((3,)),
            dma((3,)),
        ],
        compiler_params=pltpu.CompilerParams(
            collective_id=0, has_side_effects=True, vmem_limit_bytes=60 * 2**20
        ),
        name="gather_factor_panel",
    )(scaled, picked, coulomb.reshape(128, 128), pivots)


def solution(mesh):
    finer = Mesh(mesh.devices.reshape(NY, NC, NX, NZ), ("y", "c", "x", "z"))
    return jax.shard_map(
        body,
        mesh=finer,
        in_specs=(P(("x", "z"), ("y", "c")), P(("y", "c")), P(), P()),
        out_specs=(P(("y", "c"), ("x", "z")), P(("y", "c"), None)),
        check_vma=False,
    )
```

time: 588 us -> 134 us (0.23); the launches traced: 578 us -> 133 us
  waiting for transfers between devices: 314 us -> 0 us
  other arithmetic: 133 us -> 0 us
  Pallas kernels: 0 us -> 128 us
  local copies, waits for them, and re-layouts: 56 us -> 4.55 us
  matrix products: 22.4 us -> 0 us
  starting transfers between devices: 19.7 us -> 0 us
  between operations: 16.8 us -> 0.65 us
  blocking collectives: 16 us -> 0 us
    all_gather x3 -> x0, waiting for transfers between devices: 162 us -> none  [the longest x2 87 us: gather_in_order(): blocks = lax.all_gather(blocks, axes[k])]
    pallas_call x0 -> x2, Pallas kernels: none -> 128 us  [the longest x1 126 us: body(): pl.pallas_call(main_kernel, out_shape=(jax.ShapeDtypeStruct((ROWS, COLS),...]
    another operation x17 -> x0, other arithmetic: 121 us -> none  [the longest x14 78.9 us: factor_rows(): factor = jnp.linalg.cholesky(pivot_block)]
    all_to_all x2 -> x0, waiting for transfers between devices: 89.4 us -> none  [the longest x1 89.4 us: body(): lax.all_to_all(every_wave, GROW, split_axis=0, concat_axis=1, tiled=True)]
    reduce_scatter x2 -> x0, waiting for transfers between devices: 61.9 us -> none  [reduced_to_own(): blocks = lax.psum_scatter(blocks, axes[k], scatter_dimension=0, tiled=True)]
    gather x7 -> x0, local copies, waits for them, and re-layouts: 20.9 us -> none  [the longest x2 7.92 us: factor_rows(): top_rows = jnp.take(upper, position, axis=0)]
    all_to_all x2 -> x0, starting transfers between devices: 19.5 us -> none  [the longest x1 11.8 us: sent_to_all(): lax.all_to_all(jnp.broadcast_to(x[None], (length, *x.shape)), axis, 0, 0,...]
    another operation x18 -> x0, local copies, waits for them, and re-layouts: 16.8 us -> none
  transfers between devices with their start and end apart: 7 -> 0, of which waited for: 6 -> 0; matrix products, arithmetic and copies ran while one was open for 2% -> 0% of each run, Pallas kernels for 0% -> 0%
where the time goes in v1:
time: 134 us; the launch traced here: 133 us
  Pallas kernels  128 us (96%)
  local copies, waits for them, and re-layouts  4.55 us (3%)
    pallas_call x1, Pallas kernels, body(): pl.pallas_call(main_kernel, out_shape=(jax.ShapeDtypeStruct((ROWS, COLS),...  126 us
    unnamed x4, local copies, waits for them, and re-layouts  4.55 us

profile of v1, /device:TPU:1, one launch (start us, length us, event | category | flops | bytes accessed | tf_op | source)
XLA Modules:
  0.0 133.4 jit_solution(1291025084200260847)
XLA Ops:
  0.6 1.9 %scale_and_pick.1 = (bf16[512,128]{1,0:T(8,128)(2,1)}, bf16[16,128]{1,0:T(8,128)(2,1)}) custom-call(bf16[512,128]{1,0:T(8,128)(2,1)} %density_ref.1, f32[1,128]{1,0:T(1,128)} %bitcast.6, s32[4,128]{1,0:T(4,128)} %bitcast.4), custom_call_target="tpu_custom_call" | custom-call | tf_op jit(solution)/shard_map/scale_and_pick/pallas_call | solution.py:495
  2.6 126.3 %gather_factor_panel.1 = (f32[1024,512]{1,0:T(8,128)}, f32[1024,512]{1,0:T(8,128)}) custom-call(bf16[512,128]{1,0:T(8,128)(2,1)} %get-tuple-element.4.scaled_ref, bf16[16,128]{1,0:T(8,128)(2,1)} %get-tuple-element.5.picked_ref, f32[128,128]{1,0:T(8,128)} %bitcast.3, s32[4,128]{1,0:T(4,128)} %bitcast.5), custom_call_target="tpu_custom_call" | custom-call | tf_op jit(solution)/shard_map/gather_factor_panel/pallas_call | solution.py:506
  128.8 0.0 copy-start
  128.8 3.2 %copy.8 = f32[1024,512]{1,0:T(8,128)} copy(f32[1024,512]{1,0:T(8,128)} %get-tuple-element.8) | data formatting | bytes 4194304
  132.1 0.0 copy-done
  132.1 1.3 copy.9
Async XLA Ops:
  128.8 3.2 %copy-start = (f32[1024,512]{1,0:T(8,128)S(1)}, f32[1024,512]{1,0:T(8,128)}, u32[]{:S(2)}) copy-start(f32[1024,512]{1,0:T(8,128)} %get-tuple-element.9) | copy-start | bytes 6291460

commit v2 on v1

--- a/solution.py
+++ b/solution.py
@@ -117,111 +117,118 @@
     lax.fori_loop(0, 4, block, 0)
 
 
-def prologue(density_ref, weight_ref, pivots_ref, scaled_ref, picked_ref):
-    first = (lax.axis_index("x") * NZ + lax.axis_index("z")) * COLS
-    scaled = (density_ref[...].astype(f32) * jnp.sqrt(weight_ref[...])).astype(bf16)
-    scaled_ref[...] = scaled
-    pivots = column_of(jnp.concatenate([pivots_ref[i : i + 1, :] for i in range(4)], axis=1).astype(f32))
+def pick_pivots(scaled, pivot_column, first):
     waves = (first + iota((PANEL, COLS), 1)).astype(f32)
-    taken = jnp.sum(jnp.where(pivots == waves, 1.0, 0.0), axis=0, keepdims=True)
+    taken = jnp.sum(jnp.where(pivot_column == waves, 1.0, 0.0), axis=0, keepdims=True)
     in_run = iota((MINE, COLS), 1) // RUN == iota((MINE, COLS), 0)
     one_hot = jnp.where(in_run, jnp.broadcast_to(taken, (MINE, COLS)), 0.0).astype(bf16)
-    picked_ref[...] = jnp.dot(one_hot, scaled, preferred_element_type=f32).astype(bf16)
+    return jnp.dot(one_hot, scaled, preferred_element_type=f32).astype(bf16)
 
 
 class Gather:
-    def __init__(self, slot, line, sems, place):
-        self.slot, self.line, self.sems, self.place = slot, line, sems, place
-
-    def ring_z(self, view, step, base):
-        y, c, x, z = self.place
+    def __init__(self, slot, sems, place, also=None):
+        self.slot, self.sems, self.place, self.also = slot, sems, place, also
+        y, c, x, z = place
+        self.right_x, self.left_x = (y, c, lax.rem(x + 1, NX), z), (y, c, lax.rem(x + NX - 1, NX), z)
+        self.right_z, self.left_z = (y, c, x, lax.rem(z + 1, NZ)), (y, c, x, lax.rem(z + NZ - 1, NZ))
+
+    def z_at(self, j):
+        z = self.place[3]
+        return lax.rem(z + (NZ - j if j <= 4 else j - 4), NZ)
+
+    def x_at(self, i):
+        return lax.rem(self.place[2] + (0, NX - 1, 1, 2)[i], NX)
+
+    def copy(self, ref, k, device):
         send, recv = self.sems
+        return pltpu.make_async_remote_copy(ref, ref, send.at[k], recv.at[k], device, MESH_ID)
+
+    def events(self, core):
+        x, z = self.place[2], self.place[3]
+        slot = self.slot
         out = []
-        right, left = lax.rem(z + 1, NZ), lax.rem(z + NZ - 1, NZ)
-        from_left = lax.rem(z + NZ - step + 1, NZ), lax.rem(z + NZ - step, NZ)
-        k = base + 2 * (step - 1)
-        out.append((view(from_left[0]), view(from_left[1]), k, (y, c, x, right)))
-        if step < 4:
-            from_right = lax.rem(z + step - 1, NZ), lax.rem(z + step, NZ)
-            out.append((view(from_right[0]), view(from_right[1]), k + 1, (y, c, x, left)))
-        return out
-
-    def ring_x(self, view, half, step, base):
-        y, c, x, z = self.place
-        right, left = lax.rem(x + 1, NX), lax.rem(x + NX - 1, NX)
-        opposite = lax.rem(x + 2, NX)
-        k = base + 2 * (step - 1)
-        if step == 1:
-            return [
-                (view(x), view(left), k, (y, c, right, z)),
-                (view(x), view(right), k + 1, (y, c, left, z)),
-            ]
-        return [
-            (half(left, 0), half(opposite, 0), k, (y, c, right, z)),
-            (half(right, 1), half(opposite, 1), k + 1, (y, c, left, z)),
-        ]
-
-    def copies(self, core, step):
-        x, z = self.place[2], self.place[3]
         if core == 0:
-            if step < 4:
-                return self.ring_z(lambda i: self.slot(x, i), step + 1, 0)
-            return self.ring_x(
-                lambda i: self.line(0, i), lambda i, h: self.line(0, i, h), step - 3, 7
-            )
-        if step < 2:
-            return self.ring_x(
-                lambda i: self.slot(i, z), lambda i, h: self.slot(i, z, h), step + 1, 7
-            )
-        return self.ring_z(lambda i: self.line(1, i), step - 1, 0)
-
-    def each(self, core, step, do):
-        send, recv = self.sems
-        for sent, received, k, device in self.copies(core, step):
-            do(sent, received, send.at[k], recv.at[k], device)
-
-    def start(self, core, step):
-        def go(sent, received, s, r, device):
-            pltpu.make_async_remote_copy(sent, sent, s, r, device, MESH_ID).start()
-
-        self.each(core, step, go)
-
-    def wait_recv(self, core, step):
-        def go(sent, received, s, r, device):
-            pltpu.make_async_remote_copy(received, received, s, r, device, MESH_ID).wait_recv()
-
-        self.each(core, step, go)
-
-    def wait_send(self, core, step):
-        def go(sent, received, s, r, device):
-            pltpu.make_async_remote_copy(sent, sent, s, r, device, MESH_ID).wait_send()
-
-        self.each(core, step, go)
-
-    def advance(self, event):
+            own = [(slot(x, z), 1, self.right_z), (slot(x, z), 5, self.left_z)]
+            own += [(slot(x, z), 8, self.right_x), (slot(x, z), 16, self.left_x)]
+            out.append((0.0, [], own, None))
+            for j in range(1, 8):
+                here = slot(x, self.z_at(j))
+                sends = []
+                if j in (1, 2, 3, 5, 6):
+                    sends.append((here, j + 1, self.right_z if j < 4 else self.left_z))
+                sends += [(here, 8 + j, self.right_x), (here, 16 + j, self.left_x)]
+                steps = j if j <= 4 else j - 4
+                out.append((1.0 * steps, [(here, j)], sends, (x, self.z_at(j))))
+            for p, j in enumerate((0, 1, 5, 2, 6, 3, 7, 4)):
+                zz = self.z_at(j)
+                a, b, o = (self.x_at(i) for i in (1, 2, 3))
+                out.append((1.3 + p * 0.9, [(slot(a, zz), 8 + j)], [(slot(a, zz, 0), 24 + j, self.right_x)], (a, zz)))
+                out.append((1.3 + p * 0.9, [(slot(b, zz), 16 + j)], [(slot(b, zz, 1), 32 + j, self.left_x)], (b, zz)))
+                halves = [(slot(o, zz, 0), 24 + j), (slot(o, zz, 1), 32 + j)]
+                out.append((2.6 + p * 0.9, halves, [], (o, zz)))
+        else:
+
+            def along_z(i, step, side, ref):
+                k = (4 if side == 0 else 20) + 4 * (step - 1) + i
+                return (ref, k, self.right_z if side == 0 else self.left_z)
+
+            own = [(slot(x, z), 0, self.right_x), (slot(x, z), 1, self.left_x)]
+            own += [along_z(0, 1, side, slot(x, z)) for side in range(2)]
+            out.append((0.0, [], own, None))
+            for i in (1, 2, 3):
+                xx = self.x_at(i)
+                here = slot(xx, z)
+                sends = [along_z(i, 1, side, here) for side in range(2)]
+                waits = [(here, i - 1)]
+                if i < 3:
+                    sends.insert(0, (slot(xx, z, i - 1), i + 1, self.right_x if i == 1 else self.left_x))
+                else:
+                    waits = [(slot(xx, z, 0), 2), (slot(xx, z, 1), 3)]
+                out.append((1.0 if i < 3 else 2.0, waits, sends, (xx, z)))
+            for step in range(1, 5):
+                for i in range(4):
+                    for side in range(2 if step < 4 else 1):
+                        zz = self.z_at(step + 4 * side)
+                        here = slot(self.x_at(i), zz)
+                        sends = [along_z(i, step + 1, side, here)] if step + side < 4 else []
+                        k = (4 if side == 0 else 20) + 4 * (step - 1) + i
+                        when = max(1.0 * step + (0, 1, 1, 2)[i], 1.05 + 2.0 * (step - 1) + 0.5 * i)
+                        out.append((when, [(here, k)], sends, (self.x_at(i), zz)))
+        return [e[1:] for e in sorted(out, key=lambda e: e[0])]
+
+    def run(self, first, last=None):
         for core in range(2):
 
             @pl.when(self.place[1] == core)
             def _():
-                if event > 0:
-                    self.wait_recv(core, event - 1)
-                if event < 6:
-                    self.start(core, event)
+                for waits, sends, arrived in self.events(core)[first : first + 1 if last is None else last]:
+                    for ref, k in waits:
+                        self.copy(ref, k, self.right_x).wait_recv()
+                    for ref, k, device in sends:
+                        self.copy(ref, k, device).start()
+                    if self.also is not None and arrived is not None:
+                        self.also(*arrived).start()
 
     def drain(self):
         for core in range(2):
 
             @pl.when(self.place[1] == core)
             def _():
-                for step in range(6):
-                    self.wait_send(core, step)
+                for waits, sends, arrived in self.events(core):
+                    for ref, k, device in sends:
+                        self.copy(ref, k, device).wait_send()
+                    if self.also is not None and arrived is not None:
+                        self.also(*arrived).wait_send()
+
+
+EVENTS = 32
 
 
 def main_kernel(
-    scaled_ref,
-    picked_ref,
-    coulomb_ref,
-    pivots_ref,
+    density_in,
+    weight_in,
+    coulomb_in,
+    pivots_in,
     dielectric_ref,
     panel_ref,
     q_ref,
@@ -231,6 +238,12 @@
     aug,
     s_ref,
     columns_ref,
+    density_ref,
+    weight_ref,
+    coulomb_ref,
+    pivots_ref,
+    scaled_ref,
+    picked_ref,
     local_sem,
     qy_send,
     qy_recv,
@@ -242,6 +255,10 @@
     cy_recv,
     one_send,
     one_recv,
+    qx_send,
+    qx_recv,
+    cx_send,
+    cx_recv,
 ):
     y, c, x, z = (lax.axis_index(a) for a in ("y", "c", "x", "z"))
     place = (y, c, x, z)
@@ -277,27 +294,17 @@
             pl.ds(pl.multiple_of(owner_of(zz) * OWN, OWN), OWN),
         ]
 
-    def r_line(core, i, part=None):
-        if core == 0:
-            first, count = (i // 2) * COLS, COLS
-            if part is not None:
-                first, count = first + part * (COLS // 2), COLS // 2
-            return r_ref.at[lax.rem(i, 2), pl.ds(pl.multiple_of(first, 256), count), :]
-        return r_ref.at[:, :, pl.ds(pl.multiple_of(owner_of(i) * OWN, OWN), OWN)]
-
-    def q_slot(xx, zz, part=None):
+    def q_slot(xx, zz, part=None, core=None):
         rows = pl.ds(pl.multiple_of(zz * MINE, MINE), MINE)
         cols = slice(None) if part is None else pl.ds(part * (HALF // 2), HALF // 2)
-        return q_ref.at[c, xx, rows, cols]
-
-    def q_line(core, i, part=None):
-        if core == 0:
-            rows = slice(None) if part is None else pl.ds(part * 64, 64)
-            return q_ref.at[c, i, rows, :]
-        return q_ref.at[c, :, pl.ds(pl.multiple_of(i * MINE, MINE), MINE), :]
-
-    q_gather = Gather(q_slot, q_line, (qg_send, qg_recv), place)
-    r_gather = Gather(r_slot, r_line, (rg_send, rg_recv), place)
+        return q_ref.at[c if core is None else core, xx, rows, cols]
+
+    def q_pass(xx, zz, back=False):
+        ref, k = q_slot(xx, zz, core=1 - c if back else c), xx * NZ + zz
+        return pltpu.make_async_remote_copy(ref, ref, qx_send.at[k], qx_recv.at[k], partner, MESH_ID)
+
+    q_gather = Gather(q_slot, (qg_send, qg_recv), place, q_pass)
+    r_gather = Gather(r_slot, (rg_send, rg_recv), place)
 
     barrier = pltpu.get_barrier_semaphore()
     greeted = [(lax.rem(y + d, NY), c, x, z) for d in range(1, NY)]
@@ -307,12 +314,27 @@
     for device in greeted:
         pl.semaphore_signal(barrier, 1, device_id=device, device_id_type=MESH_ID)
 
-    own_q = q_ref.at[c, x, pl.ds(pl.multiple_of(z * MINE, MINE), MINE), pl.ds(pl.multiple_of(y * OWN, OWN), OWN)]
-    own_c = c_ref.at[c, :, pl.ds(pl.multiple_of(y * OWN, OWN), OWN)]
-    keep_q = pltpu.make_async_copy(picked_ref, own_q, local_sem.at[0])
-    keep_c = pltpu.make_async_copy(scaled_ref, own_c, local_sem.at[1])
-    keep_q.start()
-    keep_c.start()
+    inputs = [
+        pltpu.make_async_copy(density_in, density_ref, local_sem.at[0]),
+        pltpu.make_async_copy(weight_in, weight_ref, local_sem.at[1]),
+        pltpu.make_async_copy(pivots_in, pivots_ref, local_sem.at[2]),
+        pltpu.make_async_copy(coulomb_in, coulomb_ref, local_sem.at[3]),
+    ]
+    for copy in inputs:
+        copy.start()
+    for copy in inputs:
+        copy.wait()
+    pivot_row = jnp.concatenate([pivots_ref[i : i + 1, :] for i in range(4)], axis=1)
+    first_col = (x * NZ + z) * COLS
+    scaled = (density_ref[...].astype(f32) * jnp.sqrt(weight_ref[...])).astype(bf16)
+    picked_own = pick_pivots(scaled, column_of(pivot_row.astype(f32)), first_col)
+    own_rows = pl.ds(pl.multiple_of(z * MINE, MINE), MINE)
+    own_pairs = pl.ds(pl.multiple_of(y * OWN, OWN), OWN)
+    scaled_ref[...] = scaled
+    picked_ref[...] = picked_own
+    c_ref[c, :, own_pairs] = scaled
+    q_ref[c, x, own_rows, own_pairs] = picked_own
+    own_q = q_ref.at[c, x, own_rows, own_pairs]
     pl.semaphore_wait(barrier, len(greeted))
 
     def picked_copy(d):
@@ -323,7 +345,7 @@
 
     def picked_arrival(d):
         other = lax.rem(y + NY - d, NY)
-        there = q_ref.at[c, x, pl.ds(pl.multiple_of(z * MINE, MINE), MINE), pl.ds(pl.multiple_of(other * OWN, OWN), OWN)]
+        there = q_ref.at[c, x, own_rows, pl.ds(pl.multiple_of(other * OWN, OWN), OWN)]
         return pltpu.make_async_remote_copy(
             there, there, qy_send.at[d], qy_recv.at[d], partner, MESH_ID
         )
@@ -355,34 +377,35 @@
             ref = came if received else sent
             yield pltpu.make_async_remote_copy(ref, ref, cy_send.at[k], cy_recv.at[k], device, MESH_ID)
 
-    def half_of(ref, k):
-        ours, theirs = ref.at[c], ref.at[1 - c]
-        out = pltpu.make_async_remote_copy(ours, ours, one_send.at[k], one_recv.at[k], partner, MESH_ID)
-        back = pltpu.make_async_remote_copy(theirs, theirs, one_send.at[k], one_recv.at[k], partner, MESH_ID)
-        return out, back
-
-    q_out, q_back = half_of(q_ref, 1)
-    c_out, c_back = half_of(c_ref, 2)
+    def c_pass(owner, back=False):
+        ref = c_ref.at[1 - c if back else c, :, pl.ds(pl.multiple_of(owner * OWN, OWN), OWN)]
+        return pltpu.make_async_remote_copy(ref, ref, cx_send.at[owner], cx_recv.at[owner], partner, MESH_ID)
 
     def c_advance(event):
         if event > 1:
             for copy in c_copies(event - 1, True):
                 copy.wait_recv()
+            for away in (NY - event + 1, event - 1)[: 2 if event < 5 else 1]:
+                c_pass(lax.rem(y + away, NY)).start()
         if event < 5:
             for copy in c_copies(event, False):
                 copy.start()
-        if event == 5:
-            c_out.start()
-
-    keep_q.wait()
+
+    def repeat(count, do):
+        def step(i, carry):
+            do(i)
+            return carry
+
+        lax.fori_loop(0, count, step, 0)
+
     for d in range(1, NY):
         picked_arrival(d).wait_recv()
-    q_gather.advance(0)
+    q_gather.run(0)
+    q_pass(x, z).start()
     spread.start()
-    keep_c.wait()
+    c_pass(y).start()
     c_advance(1)
 
-    pivot_row = jnp.concatenate([pivots_ref[i : i + 1, :] for i in range(4)], axis=1)
     run_column = column_of((pivot_row // RUN).astype(f32))
     high_column = column_of((pivot_row // 128).astype(f32))
     low_column = column_of((pivot_row % 128).astype(f32))
@@ -393,12 +416,12 @@
     pivot_scale_row = row_of(pivot_scale)
     order = (run_column == iota((PANEL, PANEL), 1).astype(f32)).astype(bf16)
 
-    for event in range(1, 7):
-        q_gather.advance(event)
-        if event == 3:
-            c_advance(2)
-    q_out.start()
-    q_back.wait_recv()
+    q_gather.run(1, 20)
+    c_advance(2)
+    spread_in.wait_recv()
+    r_gather.run(0)
+    q_gather.run(20, EVENTS)
+    repeat(NX * NZ, lambda i: q_pass(i // NZ, lax.rem(i, NZ), True).wait_recv())
 
     gram = None
     for h in range(2):
@@ -411,28 +434,23 @@
     aug[:, :PANEL] = pivot_scale * pivot_scale_row * gram + unit
     aug[:, PANEL:] = unit
 
+    plan = {}
+    for event in range(1, EVENTS):
+        plan.setdefault((event - 1) * 25 // (EVENTS - 1), []).append(functools.partial(r_gather.run, event))
+    for event, at in ((3, 3), (4, 8), (5, 13)):
+        plan[at].append(functools.partial(c_advance, event))
+
     def between(k, b):
-        def at(block, event):
-            @pl.when(k == block)
-            def _():
-                event()
-
-        if b == 0:
-
-            @pl.when(k == 0)
-            def _():
-                spread_in.wait_recv()
-
-            at(0, lambda: r_gather.advance(0))
-            at(1, lambda: r_gather.advance(2))
-            at(2, lambda: r_gather.advance(4))
-            at(0, lambda: c_advance(3))
-            at(1, lambda: c_advance(5))
-        if b == 8:
-            at(0, lambda: r_gather.advance(1))
-            at(1, lambda: r_gather.advance(3))
-            at(2, lambda: r_gather.advance(5))
-            at(0, lambda: c_advance(4))
+        if b % 2:
+            return
+        for block in range(4):
+            todo = plan.get(8 * block + b // 2, ())
+            if todo:
+
+                @pl.when(k == block)
+                def _():
+                    for event in todo:
+                        event()
 
     factor_and_inverse(aug, s_ref, between)
 
@@ -442,11 +460,9 @@
     upper = jnp.where(col_i >= row_i, lt * diag, 0.0)
     aug[:, PANEL:] = aug[:, PANEL:] / diag
 
-    c_back.wait_recv()
-    r_gather.advance(6)
+    repeat(NY, lambda i: c_pass(i, True).wait_recv())
 
     first_row = (y * NC + c) * ROWS
-    first_col = (x * NZ + z) * COLS
     row_scale = jnp.sqrt(column_of(lanes_of(coulomb_ref, (y * NC + c) * 8, 8)))
     col_scale = jnp.sqrt(lanes_of(coulomb_ref, (x * NZ + z) * 4, 4))
     tile = 256
@@ -483,25 +499,14 @@
     for step in range(1, 5):
         for copy in c_copies(step, False):
             copy.wait_send()
-    q_out.wait_send()
-    c_out.wait_send()
+    q_pass(x, z).wait_send()
+    repeat(NY, lambda i: c_pass(i).wait_send())
     q_gather.drain()
     r_gather.drain()
 
 
 def body(pair_density, pair_weight, coulomb, pivot_rows):
     vmem = pl.BlockSpec(memory_space=pltpu.VMEM)
-    pivots = pivot_rows.reshape(4, 128)
-    scaled, picked = pl.pallas_call(
-        prologue,
-        out_shape=(
-            jax.ShapeDtypeStruct((COLS, OWN), bf16),
-            jax.ShapeDtypeStruct((MINE, OWN), bf16),
-        ),
-        in_specs=[vmem] * 3,
-        out_specs=(vmem, vmem),
-        name="scale_and_pick",
-    )(pair_density, pair_weight.reshape(1, OWN), pivots)
     dma = pltpu.SemaphoreType.DMA
     return pl.pallas_call(
         main_kernel,
@@ -509,7 +514,7 @@
             jax.ShapeDtypeStruct((ROWS, COLS), f32),
             jax.ShapeDtypeStruct((ROWS, PANEL), f32),
         ),
-        in_specs=[vmem] * 4,
+        in_specs=[pl.BlockSpec(memory_space=pl.ANY)] * 4,
         out_specs=(vmem, vmem),
         scratch_shapes=[
             pltpu.VMEM((2, NX, NZ * MINE, HALF), bf16),
@@ -519,23 +524,33 @@
             pltpu.VMEM((PANEL, 2 * PANEL), f32),
             pltpu.VMEM((128, 256), f32),
             pltpu.VMEM((256, PANEL), f32),
-            dma((2,)),
+            pltpu.VMEM((COLS, OWN), bf16),
+            pltpu.VMEM((1, OWN), f32),
+            pltpu.VMEM((128, 128), f32),
+            pltpu.VMEM((4, 128), jnp.int32),
+            pltpu.VMEM((COLS, OWN), bf16),
+            pltpu.VMEM((MINE, OWN), bf16),
+            dma((4,)),
             dma((NY,)),
             dma((NY,)),
-            dma((11,)),
-            dma((11,)),
-            dma((11,)),
-            dma((11,)),
+            dma((40,)),
+            dma((40,)),
+            dma((40,)),
+            dma((40,)),
             dma((7,)),
             dma((7,)),
-            dma((3,)),
-            dma((3,)),
+            dma((1,)),
+            dma((1,)),
+            dma((NX * NZ,)),
+            dma((NX * NZ,)),
+            dma((NY,)),
+            dma((NY,)),
         ],
         compiler_params=pltpu.CompilerParams(
-            collective_id=0, has_side_effects=True, vmem_limit_bytes=60 * 2**20
+            collective_id=0, has_side_effects=True, vmem_limit_bytes=40 * 2**20
         ),
         name="gather_factor_panel",
-    )(scaled, picked, coulomb.reshape(128, 128), pivots)
+    )(pair_density, pair_weight.reshape(1, OWN), coulomb.reshape(128, 128), pivot_rows.reshape(4, 128))
 
 
 def solution(mesh):

time: 134 us -> 123 us (0.918)
  Pallas kernels: 128 us -> 115 us
    pallas_call x1, Pallas kernels: 126 us -> 115 us  [body(): pl.pallas_call(main_kernel, out_shape=(jax.ShapeDtypeStruct((ROWS, COLS),...]
    pallas_call x1 -> x0, Pallas kernels: 1.93 us -> none  [body(): pl.pallas_call(prologue, out_shape=(jax.ShapeDtypeStruct((COLS, OWN), bf1...]
    unnamed x4 -> x10, local copies, waits for them, and re-layouts: 4.55 us -> 5.71 us
where the time goes in v2:
time: 123 us; the launch traced here: 121 us
  Pallas kernels  115 us (93%)
  local copies, waits for them, and re-layouts  5.71 us (5%)
    pallas_call x1, Pallas kernels, body(): pl.pallas_call(main_kernel, out_shape=(jax.ShapeDtypeStruct((ROWS, COLS),...  115 us
    unnamed x10, local copies, waits for them, and re-layouts  5.71 us

profile of v2, /device:TPU:1, one launch (start us, length us, event | category | flops | bytes accessed | tf_op | source)
XLA Modules:
  0.0 121.2 jit_solution(6406186553699983586)
XLA Ops:
  0.6 0.0 copy-start
  0.6 0.9 copy-done
  1.5 0.0 copy-start.1
  1.5 0.8 copy-done.1
  2.4 0.0 copy-start.2
  2.4 0.7 copy-done.2
  3.1 0.0 copy-start.3
  3.1 0.7 copy-done.3
  3.7 114.8 %gather_factor_panel.1 = (f32[1024,512]{1,0:T(8,128)S(1)}, f32[1024,512]{1,0:T(8,128)S(1)}) custom-call(bf16[512,128]{1,0:T(8,128)(2,1)S(1)} %copy-done, f32[1,128]{1,0:T(1,128)S(1)} %bitcast.5, f32[128,128]{1,0:T(8,128)S(1)} %bitcast.3, s32[4,128]{1,0:T(4,128)S(1)} %bitcast.4), custom_call_target="tpu_custom_call" | custom-call | tf_op jit(solution)/shard_map/gather_factor_panel/pallas_call | solution.py:511
  118.5 1.3 %copy.8 = f32[1024,512]{1,0:T(8,128)} copy(f32[1024,512]{1,0:T(8,128)S(1)} %get-tuple-element.4) | data formatting | bytes 4194304
  119.8 1.3 %copy.9 = f32[1024,512]{1,0:T(8,128)} copy(f32[1024,512]{1,0:T(8,128)S(1)} %get-tuple-element.5) | data formatting | bytes 4194304
Async XLA Ops:
  0.6 0.9 copy-start
  1.5 0.8 copy-start.1
  2.4 0.7 copy-start.2
  3.1 0.7 copy-start.3

commit v3 on v2

--- a/solution.py
+++ b/solution.py
@@ -71,46 +71,64 @@
 
 def eight_rows(s_ref, c):
     sub = iota((8, 128), 0)
-    rows = s_ref[c : c + 8, :]
-    cols = [jnp.broadcast_to(rows[:, c + j : c + j + 1], (8, 128)) for j in range(8)]
-    left, right = rows[:, :128], rows[:, 128:]
+
+    def taken(first):
+        rows = s_ref[first : first + 8, :]
+        cols = [jnp.broadcast_to(rows[:, c + j : c + j + 1], (8, 128)) for j in range(8)]
+        return [cols, rows[:, :128], rows[:, 128:]]
+
+    ahead = [first for first in (c + 8, c + 16) if first < 128]
+    cols, left, right = taken(c)
+    later = [taken(first) for first in ahead]
     for j in range(8):
         r = lax.rsqrt(jnp.broadcast_to(cols[j][j : j + 1, :], (8, 128)))
         f = jnp.where(sub > j, cols[j] * r, 0.0)
         own = jnp.where(sub == j, r, 1.0)
+        factors = [part[0][j] * r for part in later]
         for m in range(j + 1, 8):
-            cols[m] = cols[m] - f * (jnp.broadcast_to(cols[m][j : j + 1, :], (8, 128)) * r)
+            pivot = jnp.broadcast_to(cols[m][j : j + 1, :], (8, 128)) * r
+            cols[m] = cols[m] - f * pivot
+            for part, g in zip(later, factors):
+                part[0][m] = part[0][m] - g * pivot
         left_j = jnp.broadcast_to(left[j : j + 1, :], (8, 128)) * r
         right_j = jnp.broadcast_to(right[j : j + 1, :], (8, 128)) * r
         left = left * own - f * left_j
         right = right * own - f * right_j
+        for part, g in zip(later, factors):
+            part[1] = part[1] - g * left_j
+            part[2] = part[2] - g * right_j
     y = jnp.concatenate([left, right], axis=1)
     s_ref[c : c + 8, :] = y
-    if c + 8 < 128:
+    for first, part in zip(ahead, later):
+        s_ref[first : first + 8, :] = jnp.concatenate(part[1:], axis=1)
+    rest = c + 24
+    if rest < 128:
         h, m, l = split3(y)
         lhs = jnp.concatenate([h, h, m, h, l, m], axis=0)[:, :128].astype(bf16)
         rhs = jnp.concatenate([h, m, h, l, h, m], axis=0).astype(bf16)
-        s_ref[c + 8 :, :] = s_ref[c + 8 :, :] - t_times(lhs, rhs)[c + 8 :, :]
+        s_ref[rest:, :] = s_ref[rest:, :] - t_times(lhs, rhs)[rest:, :]
 
 
 def factor_and_inverse(aug, s_ref, between):
     def block(k, carry):
         o = pl.multiple_of(k * 128, 128)
+        span = pl.ds(o, PANEL + 128)
         s_ref[:, :128] = aug[pl.ds(o, 128), pl.ds(o, 128)]
         s_ref[:, 128:] = eye(128).astype(f32)
         for b in range(16):
+            if b % 4 == 0:
+                between(k, b // 4)
             eight_rows(s_ref, 8 * b)
-            between(k, b)
-        aug[pl.ds(o, 128), :] = jnp.dot(
-            s_ref[:, 128:], aug[pl.ds(o, 128), :], precision=HI, preferred_element_type=f32
+        aug[pl.ds(o, 128), span] = jnp.dot(
+            s_ref[:, 128:], aug[pl.ds(o, 128), span], precision=HI, preferred_element_type=f32
         )
         for i in range(1, 4):
 
             @pl.when(i > k)
             def _():
                 lhs = aug[pl.ds(o, 128), i * 128 : (i + 1) * 128]
-                update = t_times(lhs, aug[pl.ds(o, 128), :], HI)
-                aug[i * 128 : (i + 1) * 128, :] = aug[i * 128 : (i + 1) * 128, :] - update
+                update = t_times(lhs, aug[pl.ds(o, 128), span], HI)
+                aug[i * 128 : (i + 1) * 128, span] = aug[i * 128 : (i + 1) * 128, span] - update
 
         return carry
 
@@ -126,11 +144,19 @@
 
 
 class Gather:
-    def __init__(self, slot, sems, place, also=None):
-        self.slot, self.sems, self.place, self.also = slot, sems, place, also
+    def __init__(self, sems, place):
+        self.sems, self.place = sems, place
         y, c, x, z = place
-        self.right_x, self.left_x = (y, c, lax.rem(x + 1, NX), z), (y, c, lax.rem(x + NX - 1, NX), z)
-        self.right_z, self.left_z = (y, c, x, lax.rem(z + 1, NZ)), (y, c, x, lax.rem(z + NZ - 1, NZ))
+        self.right_x, self.left_x = self.to_x(1), self.to_x(NX - 1)
+        self.right_z, self.left_z = self.to_z(1), self.to_z(NZ - 1)
+
+    def to_x(self, d):
+        y, c, x, z = self.place
+        return (y, c, lax.rem(x + d, NX), z)
+
+    def to_z(self, d):
+        y, c, x, z = self.place
+        return (y, c, x, lax.rem(z + d, NZ))
 
     def z_at(self, j):
         z = self.place[3]
@@ -143,82 +169,174 @@
         send, recv = self.sems
         return pltpu.make_async_remote_copy(ref, ref, send.at[k], recv.at[k], device, MESH_ID)
 
+    def run(self, first, last=None):
+        for core in range(2):
+
+            @pl.when(self.place[1] == core)
+            def _():
+                for waits, sends, passes in self.events(core)[first : first + 1 if last is None else last]:
+                    for ref, k in waits:
+                        self.copy(ref, k, self.right_x).wait_recv()
+                    for ref, k, device in sends:
+                        self.copy(ref, k, device).start()
+                    for line in passes:
+                        self.line(*line).start()
+
+    def drain(self):
+        for core in range(2):
+
+            @pl.when(self.place[1] == core)
+            def _():
+                for waits, sends, passes in self.events(core):
+                    for ref, k, device in sends:
+                        self.copy(ref, k, device).wait_send()
+                    for line in passes:
+                        self.line(*line).wait_send()
+
+
+class PivotGather(Gather):
+    def __init__(self, q_ref, sems, pass_sems, place):
+        super().__init__(sems, place)
+        self.q_ref, self.pass_sems = q_ref, pass_sems
+
+    def at(self, xs, z=None, core=None, rows=None):
+        if z is not None:
+            rows = pl.ds(pl.multiple_of(z * MINE, MINE), MINE)
+        return self.q_ref.at[self.place[1] if core is None else core, xs, slice(None) if rows is None else rows, :]
+
+    def passed(self, ref, k):
+        send, recv = self.pass_sems
+        y, c, x, z = self.place
+        return pltpu.make_async_remote_copy(ref, ref, send.at[k], recv.at[k], (y, 1 - c, x, z), MESH_ID)
+
+    def line(self, core, i, back=False):
+        owner = 1 - self.place[1] if back else self.place[1]
+        return self.passed(self.at(i, core=owner) if core == 0 else self.at(slice(None), i, core=owner), i)
+
+    def wait_passed(self):
+        for core in range(2):
+
+            @pl.when(self.place[1] == core)
+            def _():
+                def step(i, carry):
+                    self.line(1 - core, i, True).wait_recv()
+                    return carry
+
+                lax.fori_loop(0, NZ if core == 0 else NX, step, 0)
+
     def events(self, core):
-        x, z = self.place[2], self.place[3]
+        x, z = self.place[2:]
+        everything = slice(None)
+        if core == 0:
+            start = [(self.at(x, z), d, self.to_z(d)) for d in (4, 3, 5, 2, 6, 1, 7)]
+            arrive = [(self.at(x, lax.rem(z + NZ - d, NZ)), d) for d in range(1, NZ)]
+            mine, a, b, o = (self.x_at(i) for i in range(4))
+            whole = [(self.at(mine), 8, self.right_x), (self.at(mine), 9, self.left_x)]
+            low, high = pl.ds(0, 64), pl.ds(64, 64)
+            first = ([(self.at(a), 8)], [(self.at(a, rows=low), 10, self.right_x)], [(0, a)])
+            second = ([(self.at(b), 9)], [(self.at(b, rows=high), 11, self.left_x)], [(0, b)])
+            both = [(self.at(o, rows=low), 10), (self.at(o, rows=high), 11)]
+            none = ([], [], [])
+            return [([], start, []), none, none, (arrive, whole, [(0, mine)]), none, first, second, none, (both, [], [(0, o)])]
+
+        def part(zz, m):
+            return self.at(pl.ds(2 * m, 2), zz)
+
+        def key(step, m, side):
+            return 4 + 4 * (step - 1) + 2 * m + side
+
+        def onward(step, zz, m):
+            out = []
+            if step < 4 or m == 0:
+                out.append((part(zz[0], m), key(step, m, 0), self.right_z))
+            if step < 4 or m == 1:
+                out.append((part(zz[1], m), key(step, m, 1), self.left_z))
+            return out
+
+        start = [(self.at(x, z), d, self.to_x(d)) for d in (2, 1, 3)]
+        arrive = [(self.at(lax.rem(x + NX - d, NX), z), d) for d in range(1, NX)]
+        out = [([], start, []), (arrive, onward(1, (z, z), 0) + onward(1, (z, z), 1), [(1, z)])]
+        for step in (1, 2, 3):
+            zz = self.z_at(step), self.z_at(step + 4)
+            for m in range(2):
+                waits = [(part(zz[side], m), key(step, m, side)) for side in range(2)]
+                out.append((waits, onward(step + 1, zz, m), [(1, zz[side]) for side in range(2)] if m else []))
+        far = self.z_at(4)
+        out.append(([(part(far, 0), key(4, 0, 0)), (part(far, 1), key(4, 1, 1))], [], [(1, far)]))
+        return out
+
+
+class RowGather(Gather):
+    RIGHT = ((1, 0), (2, 0), (1, 1), (1, 2), (1, 3), (3, 0), (2, 1), (2, 2), (2, 3), (4, 0), (3, 1), (3, 2), (3, 3), (4, 1))
+    LEFT = ((1, 0), (2, 0), (1, 1), (1, 2), (1, 3), (3, 0), (2, 1), (2, 2), (2, 3), (3, 1), (3, 2), (4, 2), (3, 3), (4, 3))
+
+    def __init__(self, slot, sems, place):
+        super().__init__(sems, place)
+        self.slot = slot
+
+    def events(self, core):
+        x, z = self.place[2:]
         slot = self.slot
         out = []
         if core == 0:
             own = [(slot(x, z), 1, self.right_z), (slot(x, z), 5, self.left_z)]
             own += [(slot(x, z), 8, self.right_x), (slot(x, z), 16, self.left_x)]
-            out.append((0.0, [], own, None))
-            for j in range(1, 8):
+            out.append(([], own, []))
+            order = (0, 1, 5, 2, 6, 3, 7, 4)
+
+            def along_z(j):
                 here = slot(x, self.z_at(j))
-                sends = []
-                if j in (1, 2, 3, 5, 6):
-                    sends.append((here, j + 1, self.right_z if j < 4 else self.left_z))
-                sends += [(here, 8 + j, self.right_x), (here, 16 + j, self.left_x)]
-                steps = j if j <= 4 else j - 4
-                out.append((1.0 * steps, [(here, j)], sends, (x, self.z_at(j))))
-            for p, j in enumerate((0, 1, 5, 2, 6, 3, 7, 4)):
-                zz = self.z_at(j)
-                a, b, o = (self.x_at(i) for i in (1, 2, 3))
-                out.append((1.3 + p * 0.9, [(slot(a, zz), 8 + j)], [(slot(a, zz, 0), 24 + j, self.right_x)], (a, zz)))
-                out.append((1.3 + p * 0.9, [(slot(b, zz), 16 + j)], [(slot(b, zz, 1), 32 + j, self.left_x)], (b, zz)))
-                halves = [(slot(o, zz, 0), 24 + j), (slot(o, zz, 1), 32 + j)]
-                out.append((2.6 + p * 0.9, halves, [], (o, zz)))
-        else:
-
-            def along_z(i, step, side, ref):
-                k = (4 if side == 0 else 20) + 4 * (step - 1) + i
-                return (ref, k, self.right_z if side == 0 else self.left_z)
-
-            own = [(slot(x, z), 0, self.right_x), (slot(x, z), 1, self.left_x)]
-            own += [along_z(0, 1, side, slot(x, z)) for side in range(2)]
-            out.append((0.0, [], own, None))
-            for i in (1, 2, 3):
-                xx = self.x_at(i)
-                here = slot(xx, z)
-                sends = [along_z(i, 1, side, here) for side in range(2)]
-                waits = [(here, i - 1)]
-                if i < 3:
-                    sends.insert(0, (slot(xx, z, i - 1), i + 1, self.right_x if i == 1 else self.left_x))
+                waits, sends = [(here, j)], []
+                if j == 4:
+                    waits = [(slot(x, self.z_at(4), 0), 4), (slot(x, self.z_at(4), 1), 32)]
+                elif j == 3:
+                    sends = [(slot(x, self.z_at(3), 0), 4, self.right_z)]
+                elif j == 7:
+                    sends = [(slot(x, self.z_at(7), 1), 32, self.left_z)]
                 else:
-                    waits = [(slot(xx, z, 0), 2), (slot(xx, z, 1), 3)]
-                out.append((1.0 if i < 3 else 2.0, waits, sends, (xx, z)))
-            for step in range(1, 5):
-                for i in range(4):
-                    for side in range(2 if step < 4 else 1):
-                        zz = self.z_at(step + 4 * side)
-                        here = slot(self.x_at(i), zz)
-                        sends = [along_z(i, step + 1, side, here)] if step + side < 4 else []
-                        k = (4 if side == 0 else 20) + 4 * (step - 1) + i
-                        when = max(1.0 * step + (0, 1, 1, 2)[i], 1.05 + 2.0 * (step - 1) + 0.5 * i)
-                        out.append((when, [(here, k)], sends, (self.x_at(i), zz)))
-        return [e[1:] for e in sorted(out, key=lambda e: e[0])]
-
-    def run(self, first, last=None):
-        for core in range(2):
-
-            @pl.when(self.place[1] == core)
-            def _():
-                for waits, sends, arrived in self.events(core)[first : first + 1 if last is None else last]:
-                    for ref, k in waits:
-                        self.copy(ref, k, self.right_x).wait_recv()
-                    for ref, k, device in sends:
-                        self.copy(ref, k, device).start()
-                    if self.also is not None and arrived is not None:
-                        self.also(*arrived).start()
-
-    def drain(self):
-        for core in range(2):
-
-            @pl.when(self.place[1] == core)
-            def _():
-                for waits, sends, arrived in self.events(core):
-                    for ref, k, device in sends:
-                        self.copy(ref, k, device).wait_send()
-                    if self.also is not None and arrived is not None:
-                        self.also(*arrived).wait_send()
+                    sends = [(here, j + 1, self.right_z if j < 4 else self.left_z)]
+                return waits, sends + [(here, 8 + j, self.right_x), (here, 16 + j, self.left_x)], []
+
+            def along_x(p, side):
+                j = order[p]
+                here = slot(self.x_at(1 + side), self.z_at(j) if j else z)
+                sends = [(here, 24 + j, self.left_x if side else self.right_x)] if p % 2 == side else []
+                return [(here, (16 if side else 8) + j)], sends, []
+
+            def opposite(p):
+                j = order[p]
+                return [(slot(self.x_at(3), self.z_at(j) if j else z), 24 + j)], [], []
+
+            out += [along_z(1), along_z(5), along_x(0, 0), along_x(0, 1), along_z(2), along_z(6)]
+            out += [along_x(1, 0), along_x(1, 1), opposite(0), along_z(3), along_z(7)]
+            out += [along_x(2, 0), along_x(2, 1), opposite(1), along_z(4)]
+            for p in range(3, 8):
+                out += [along_x(p, 0), along_x(p, 1), opposite(p - 1)]
+            out.append(opposite(7))
+            return out
+
+        def key(step, i, side):
+            return 4 + 8 * (step - 1) + 2 * i + side
+
+        def onward(step, i, side, here):
+            if step > 4 or (step == 4 and i // 2 != side):
+                return []
+            return [(here, key(step, i, side), self.left_z if side else self.right_z)]
+
+        def along(step, i, side):
+            here = slot(self.x_at(i), self.z_at(step + 4 * side if step < 4 else 4))
+            return [(here, key(step, i, side))], onward(step + 1, i, side, here), []
+
+        own = [(slot(x, z), d, self.to_x(d)) for d in (2, 1, 3)]
+        out.append(([], own + onward(1, 0, 0, slot(x, z)) + onward(1, 0, 1, slot(x, z)), []))
+        right, left = list(self.RIGHT), list(self.LEFT)
+        out += [along(*right.pop(0), 0), along(*left.pop(0), 1)]
+        for i, d in ((1, 1), (2, 3), (3, 2)):
+            here = slot(self.x_at(i), z)
+            out.append(([(here, d)], onward(1, i, 0, here) + onward(1, i, 1, here), []))
+        while right:
+            out += [along(*right.pop(0), 0), along(*left.pop(0), 1)]
+        return out
 
 
 EVENTS = 32
@@ -294,22 +412,13 @@
             pl.ds(pl.multiple_of(owner_of(zz) * OWN, OWN), OWN),
         ]
 
-    def q_slot(xx, zz, part=None, core=None):
-        rows = pl.ds(pl.multiple_of(zz * MINE, MINE), MINE)
-        cols = slice(None) if part is None else pl.ds(part * (HALF // 2), HALF // 2)
-        return q_ref.at[c if core is None else core, xx, rows, cols]
-
-    def q_pass(xx, zz, back=False):
-        ref, k = q_slot(xx, zz, core=1 - c if back else c), xx * NZ + zz
-        return pltpu.make_async_remote_copy(ref, ref, qx_send.at[k], qx_recv.at[k], partner, MESH_ID)
-
-    q_gather = Gather(q_slot, (qg_send, qg_recv), place, q_pass)
-    r_gather = Gather(r_slot, (rg_send, rg_recv), place)
+    q_gather = PivotGather(q_ref, (qg_send, qg_recv), (qx_send, qx_recv), place)
+    r_gather = RowGather(r_slot, (rg_send, rg_recv), place)
 
     barrier = pltpu.get_barrier_semaphore()
     greeted = [(lax.rem(y + d, NY), c, x, z) for d in range(1, NY)]
-    greeted += [(y, c, x, lax.rem(z + d, NZ)) for d in (1, NZ - 1)]
-    greeted += [(y, c, lax.rem(x + d, NX), z) for d in (1, NX - 1)]
+    greeted += [(y, c, x, lax.rem(z + d, NZ)) for d in range(1, NZ)]
+    greeted += [(y, c, lax.rem(x + d, NX), z) for d in range(1, NX)]
     greeted += [partner, target, origin]
     for device in greeted:
         pl.semaphore_signal(barrier, 1, device_id=device, device_id_type=MESH_ID)
@@ -398,10 +507,6 @@
 
         lax.fori_loop(0, count, step, 0)
 
-    for d in range(1, NY):
-        picked_arrival(d).wait_recv()
-    q_gather.run(0)
-    q_pass(x, z).start()
     spread.start()
     c_pass(y).start()
     c_advance(1)
@@ -416,12 +521,22 @@
     pivot_scale_row = row_of(pivot_scale)
     order = (run_column == iota((PANEL, PANEL), 1).astype(f32)).astype(bf16)
 
-    q_gather.run(1, 20)
+    for d in range(1, NY):
+        picked_arrival(d).wait_recv()
+    q_gather.run(0)
     c_advance(2)
+    q_gather.run(1, 3)
     spread_in.wait_recv()
     r_gather.run(0)
-    q_gather.run(20, EVENTS)
-    repeat(NX * NZ, lambda i: q_pass(i // NZ, lax.rem(i, NZ), True).wait_recv())
+    q_gather.run(3)
+    c_advance(3)
+    q_gather.run(4, 6)
+    r_gather.run(1, 3)
+    q_gather.run(6)
+    c_advance(4)
+    r_gather.run(3, 5)
+    q_gather.run(7, 9)
+    q_gather.wait_passed()
 
     gram = None
     for h in range(2):
@@ -433,32 +548,40 @@
     unit = eye(PANEL).astype(f32)
     aug[:, :PANEL] = pivot_scale * pivot_scale_row * gram + unit
     aug[:, PANEL:] = unit
-
-    plan = {}
-    for event in range(1, EVENTS):
-        plan.setdefault((event - 1) * 25 // (EVENTS - 1), []).append(functools.partial(r_gather.run, event))
-    for event, at in ((3, 3), (4, 8), (5, 13)):
-        plan[at].append(functools.partial(c_advance, event))
-
-    def between(k, b):
-        if b % 2:
-            return
+    r_gather.run(5, 11)
+    c_advance(5)
+
+    def between(k, part):
         for block in range(4):
-            todo = plan.get(8 * block + b // 2, ())
-            if todo:
+            at = 4 * block + part
+            first, last = (min(EVENTS, 11 + (21 * i) // 13) for i in (at, at + 1))
+            if first < last:
 
                 @pl.when(k == block)
                 def _():
-                    for event in todo:
-                        event()
+                    r_gather.run(first, last)
 
     factor_and_inverse(aug, s_ref, between)
 
-    lt = aug[:, :PANEL]
-    row_i, col_i = iota((PANEL, PANEL), 0), iota((PANEL, PANEL), 1)
-    diag = jnp.sum(jnp.where(row_i == col_i, lt, 0.0), axis=1, keepdims=True)
-    upper = jnp.where(col_i >= row_i, lt * diag, 0.0)
+    diag = jnp.concatenate(
+        [
+            jnp.sum(jnp.where(eye(128), aug[i : i + 128, i : i + 128], 0.0), axis=1, keepdims=True)
+            for i in range(0, PANEL, 128)
+        ],
+        axis=0,
+    )
     aug[:, PANEL:] = aug[:, PANEL:] / diag
+
+    runs = ROWS // RUN
+    run_row = pivot_row // RUN
+    pick = (run_row == (y * NC + c) * runs + iota((runs, PANEL), 0)).astype(f32)
+    top = None
+    for part in split3(aug[:, :PANEL]):
+        rows = jnp.dot(pick.astype(bf16), part.astype(bf16), preferred_element_type=f32)
+        top = rows if top is None else top + rows
+    top = top * jnp.sum(pick * row_of(diag), axis=1, keepdims=True)
+    position = jnp.sum(pick * iota((runs, PANEL), 1).astype(f32), axis=1, keepdims=True)
+    within = jnp.sum(pick * (pivot_row % RUN).astype(f32), axis=1, keepdims=True)
 
     repeat(NY, lambda i: c_pass(i, True).wait_recv())
 
@@ -479,13 +602,6 @@
         panel_ref[rows, :256] = times_t(columns_ref[:, :256], aug[:256, PANEL : PANEL + 256], HI)
         panel_ref[rows, 256:] = times_t(columns_ref[...], aug[256:, PANEL:], HI)
 
-    runs = ROWS // RUN
-    run_row = pivot_row // RUN
-    mine_here = run_row == (y * NC + c) * runs + iota((runs, PANEL), 0)
-    pick = mine_here.astype(f32)
-    top = jnp.dot(pick, upper, precision=HI, preferred_element_type=f32)
-    position = jnp.sum(pick * iota((runs, PANEL), 1).astype(f32), axis=1, keepdims=True)
-    within = jnp.sum(pick * jnp.broadcast_to((pivot_row % RUN).astype(f32), (runs, PANEL)), axis=1, keepdims=True)
     lane = iota((RUN, PANEL), 1).astype(f32)
     line = iota((RUN, PANEL), 0).astype(f32)
     for q in range(runs):
@@ -499,7 +615,6 @@
     for step in range(1, 5):
         for copy in c_copies(step, False):
             copy.wait_send()
-    q_pass(x, z).wait_send()
     repeat(NY, lambda i: c_pass(i).wait_send())
     q_gather.drain()
     r_gather.drain()
@@ -533,16 +648,16 @@
             dma((4,)),
             dma((NY,)),
             dma((NY,)),
-            dma((40,)),
-            dma((40,)),
-            dma((40,)),
-            dma((40,)),
+            dma((20,)),
+            dma((20,)),
+            dma((36,)),
+            dma((36,)),
             dma((7,)),
             dma((7,)),
             dma((1,)),
             dma((1,)),
-            dma((NX * NZ,)),
-            dma((NX * NZ,)),
+            dma((NZ,)),
+            dma((NZ,)),
             dma((NY,)),
             dma((NY,)),
         ],

time: 123 us -> 112 us (0.911)
  the two profiles are of different devices: /device:TPU:1 before, /device:TPU:38 now
where the time goes in v3:
time: 112 us
  Pallas kernels  105 us (94%)
  local copies, waits for them, and re-layouts  5.71 us (5%)
    pallas_call x1, Pallas kernels, body(): pl.pallas_call(main_kernel, out_shape=(jax.ShapeDtypeStruct((ROWS, COLS),...  105 us
    unnamed x10, local copies, waits for them, and re-layouts  5.71 us

profile of v3, /device:TPU:38, one launch (start us, length us, event | category | flops | bytes accessed | tf_op | source)
XLA Modules:
  0.0 111.5 jit_solution(1695651832148732904)
XLA Ops:
  0.6 0.0 copy-start
  0.6 0.9 copy-done
  1.5 0.0 copy-start.1
  1.5 0.8 copy-done.1
  2.4 0.0 copy-start.2
  2.4 0.7 copy-done.2
  3.1 0.0 copy-start.3
  3.1 0.7 copy-done.3
  3.7 105.1 %gather_factor_panel.1 = (f32[1024,512]{1,0:T(8,128)S(1)}, f32[1024,512]{1,0:T(8,128)S(1)}) custom-call(bf16[512,128]{1,0:T(8,128)(2,1)S(1)} %copy-done, f32[1,128]{1,0:T(1,128)S(1)} %bitcast.5, f32[128,128]{1,0:T(8,128)S(1)} %bitcast.3, s32[4,128]{1,0:T(4,128)S(1)} %bitcast.4), custom_call_target="tpu_custom_call" | custom-call | tf_op jit(solution)/shard_map/gather_factor_panel/pallas_call | solution.py:626
  108.9 1.3 %copy.8 = f32[1024,512]{1,0:T(8,128)} copy(f32[1024,512]{1,0:T(8,128)S(1)} %get-tuple-element.4) | data formatting | bytes 4194304
  110.2 1.3 %copy.9 = f32[1024,512]{1,0:T(8,128)} copy(f32[1024,512]{1,0:T(8,128)S(1)} %get-tuple-element.5) | data formatting | bytes 4194304
Async XLA Ops:
  0.6 0.9 copy-start
  1.5 0.8 copy-start.1
  2.4 0.7 copy-start.2
  3.1 0.7 copy-start.3

commit v4 on v3

--- a/solution.py
+++ b/solution.py
@@ -174,13 +174,23 @@
 
             @pl.when(self.place[1] == core)
             def _():
-                for waits, sends, passes in self.events(core)[first : first + 1 if last is None else last]:
-                    for ref, k in waits:
-                        self.copy(ref, k, self.right_x).wait_recv()
-                    for ref, k, device in sends:
-                        self.copy(ref, k, device).start()
-                    for line in passes:
-                        self.line(*line).start()
+                self.process(self.events(core)[first : first + 1 if last is None else last])
+
+    def process(self, events):
+        for waits, sends, passes in events:
+            for ref, k in waits:
+                self.copy(ref, k, self.right_x).wait_recv()
+            for ref, k, device in sends:
+                self.copy(ref, k, device).start()
+            for line in passes:
+                self.line(*line).start()
+
+    def run_core(self, core, first, last):
+        if first < last:
+
+            @pl.when(self.place[1] == core)
+            def _():
+                self.process(self.events(core)[first:last])
 
     def drain(self):
         for core in range(2):
@@ -362,6 +372,7 @@
     pivots_ref,
     scaled_ref,
     picked_ref,
+    mid_ref,
     local_sem,
     qy_send,
     qy_recv,
@@ -382,18 +393,19 @@
     place = (y, c, x, z)
     partner = (y, 1 - c, x, z)
 
-    def shift(plane, core):
-        return lax.rem(plane + 12 - 4 * lax.rem(plane, 2) - 2 * core, NY)
-
     to_y, to_c = 2 * x + z // 4, lax.rem(z // 2, 2)
-    to_half = lax.rem(z, 2)
-    target = (to_y, to_c, 2 * to_half + c, lax.rem(y + NZ - shift(to_y, to_c), NZ))
-    mine = shift(y, c)
-
-    def owner_of(zz):
-        return lax.rem(zz + mine, NY)
-
-    origin = (owner_of(z), lax.rem(x, 2), y // 2, 4 * lax.rem(y, 2) + 2 * c + x // 2)
+    mid_x, mid_z = 2 * lax.rem(z, 2) + c, lax.rem(y + 4 * c + 8 - to_y + 4 * (z // 4) + 2 * to_c, NZ)
+    middle = (y, to_c, mid_x, mid_z)
+    stays = (mid_x == x) & (mid_z == z) & (to_c == c)
+
+    turn = lax.rem(y + 4 * lax.rem(x, 2) + 2 * c + 8 - z, NZ)
+    odd = lax.rem(turn, 2)
+    origin = (y, lax.rem(x, 2), lax.rem(turn + 3 * odd, 8) // 2, 4 * odd + 2 * c + x // 2)
+    last_y = lax.rem(turn + 4 * odd, NY)
+    arrives = last_y == y
+
+    def owner_of(xx, zz):
+        return lax.rem(zz + y + 16 - 4 * lax.rem(y, 2) - 2 * c + 4 * lax.rem(xx, 2), NY)
 
     def r_block(pair_core, half, owner):
         return r_ref.at[
@@ -409,7 +421,7 @@
         return r_ref.at[
             lax.rem(xx, 2),
             pl.ds(pl.multiple_of(first, 256), count),
-            pl.ds(pl.multiple_of(owner_of(zz) * OWN, OWN), OWN),
+            pl.ds(pl.multiple_of(owner_of(xx, zz) * OWN, OWN), OWN),
         ]
 
     q_gather = PivotGather(q_ref, (qg_send, qg_recv), (qx_send, qx_recv), place)
@@ -419,7 +431,7 @@
     greeted = [(lax.rem(y + d, NY), c, x, z) for d in range(1, NY)]
     greeted += [(y, c, x, lax.rem(z + d, NZ)) for d in range(1, NZ)]
     greeted += [(y, c, lax.rem(x + d, NX), z) for d in range(1, NX)]
-    greeted += [partner, target, origin]
+    greeted += [partner, middle, origin]
     for device in greeted:
         pl.semaphore_signal(barrier, 1, device_id=device, device_id_type=MESH_ID)
 
@@ -462,13 +474,21 @@
     for d in (4, 3, 5, 2, 6, 1, 7):
         picked_copy(d).start()
 
-    spread = pltpu.make_async_remote_copy(
-        scaled_ref, r_block(c, to_half, y), one_send.at[0], one_recv.at[0], target, MESH_ID
-    )
-    arrived = r_slot(x, z)
-    spread_in = pltpu.make_async_remote_copy(
-        arrived, arrived, one_send.at[0], one_recv.at[0], origin, MESH_ID
-    )
+    away = pltpu.make_async_remote_copy(scaled_ref, mid_ref, one_send.at[0], one_recv.at[0], middle, MESH_ID)
+    stay = pltpu.make_async_copy(scaled_ref, mid_ref, local_sem.at[0])
+    here = r_slot(x, z)
+    there = r_block(lax.rem(x, 2), x // 2, y)
+    onward = pltpu.make_async_remote_copy(mid_ref, there, one_send.at[1], one_recv.at[1], (last_y, c, x, z), MESH_ID)
+    onward_in = pltpu.make_async_remote_copy(here, here, one_send.at[1], one_recv.at[1], partner, MESH_ID)
+    keep = pltpu.make_async_copy(mid_ref, here, local_sem.at[1])
+
+    def either(condition, yes, no):
+        pl.when(condition)(yes)
+        pl.when(jnp.logical_not(condition))(no)
+
+    def second_move():
+        either(stays, stay.wait, away.wait_recv)
+        either(arrives, keep.start, onward.start)
 
     def c_of(owner):
         return c_ref.at[c, :, pl.ds(pl.multiple_of(owner * OWN, OWN), OWN)]
@@ -507,7 +527,7 @@
 
         lax.fori_loop(0, count, step, 0)
 
-    spread.start()
+    either(stays, stay.start, away.start)
     c_pass(y).start()
     c_advance(1)
 
@@ -525,16 +545,16 @@
         picked_arrival(d).wait_recv()
     q_gather.run(0)
     c_advance(2)
-    q_gather.run(1, 3)
-    spread_in.wait_recv()
+    q_gather.run(1)
+    second_move()
+    q_gather.run(2, 4)
+    c_advance(3)
+    q_gather.run(4)
+    either(arrives, keep.wait, onward_in.wait_recv)
     r_gather.run(0)
-    q_gather.run(3)
-    c_advance(3)
-    q_gather.run(4, 6)
+    q_gather.run(5, 7)
+    c_advance(4)
     r_gather.run(1, 3)
-    q_gather.run(6)
-    c_advance(4)
-    r_gather.run(3, 5)
     q_gather.run(7, 9)
     q_gather.wait_passed()
 
@@ -548,18 +568,15 @@
     unit = eye(PANEL).astype(f32)
     aug[:, :PANEL] = pivot_scale * pivot_scale_row * gram + unit
     aug[:, PANEL:] = unit
-    r_gather.run(5, 11)
+    r_gather.run(3, 7)
     c_advance(5)
 
     def between(k, part):
         for block in range(4):
-            at = 4 * block + part
-            first, last = (min(EVENTS, 11 + (21 * i) // 13) for i in (at, at + 1))
-            if first < last:
-
-                @pl.when(k == block)
-                def _():
-                    r_gather.run(first, last)
+
+            @pl.when(k == block)
+            def _():
+                r_gather.run(7 + 4 * block + part)
 
     factor_and_inverse(aug, s_ref, between)
 
@@ -589,18 +606,44 @@
     row_scale = jnp.sqrt(column_of(lanes_of(coulomb_ref, (y * NC + c) * 8, 8)))
     col_scale = jnp.sqrt(lanes_of(coulomb_ref, (x * NZ + z) * 4, 4))
     tile = 256
-    for t in range(ROWS // tile):
-        rows = slice(t * tile, (t + 1) * tile)
-        scale = row_scale[rows]
-        numbers = first_row + t * tile + iota((tile, COLS), 0)
-        gram = times_t(r_ref[0, rows, :], c_ref[0]) + times_t(r_ref[1, rows, :], c_ref[1])
-        same = numbers == first_col + iota((tile, COLS), 1)
-        dielectric_ref[rows, :] = scale * col_scale * gram + jnp.where(same, 1.0, 0.0)
-        gram = times_t(r_ref[0, rows, :], qp_ref[0]) + times_t(r_ref[1, rows, :], qp_ref[1])
-        same = numbers == pivot_row
-        columns_ref[...] = scale * pivot_scale_row * gram + jnp.where(same, 1.0, 0.0)
-        panel_ref[rows, :256] = times_t(columns_ref[:, :256], aug[:256, PANEL : PANEL + 256], HI)
-        panel_ref[rows, 256:] = times_t(columns_ref[...], aug[256:, PANEL:], HI)
+
+    def product(ref, rows, wanted):
+        parts = []
+        for j in wanted:
+            zz = r_gather.z_at(j) if j else z
+            for xx in range(2):
+                owner = pl.multiple_of(owner_of(xx, zz) * OWN, OWN)
+                parts.append(ref[xx, rows, pl.ds(owner, OWN)])
+        return jnp.concatenate(parts, axis=1)
+
+    done = [23, 23]
+    groups = ((0, 1, 5, 2), (6, 3), (7, 4))
+    ready = {0: (21, 27, 31), 1: (20, 28, 31)}
+    for g, wanted in enumerate(groups):
+        for core in range(2):
+            r_gather.run_core(core, done[core], ready[core][g] + 1)
+            done[core] = max(done[core], ready[core][g] + 1)
+        everything = slice(None)
+        c_part, q_part = product(c_ref, everything, wanted), product(qp_ref, everything, wanted)
+        for t in range(ROWS // tile):
+            rows = slice(t * tile, (t + 1) * tile)
+            r_part = product(r_ref, rows, wanted)
+            gram, columns = times_t(r_part, c_part), times_t(r_part, q_part)
+            if g == 0:
+                dielectric_ref[rows, :], panel_ref[rows, :] = gram, columns
+                continue
+            gram, columns = dielectric_ref[rows, :] + gram, panel_ref[rows, :] + columns
+            if g < len(groups) - 1:
+                dielectric_ref[rows, :], panel_ref[rows, :] = gram, columns
+                continue
+            scale = row_scale[rows]
+            numbers = first_row + t * tile + iota((tile, COLS), 0)
+            same = numbers == first_col + iota((tile, COLS), 1)
+            dielectric_ref[rows, :] = scale * col_scale * gram + jnp.where(same, 1.0, 0.0)
+            same = numbers == pivot_row
+            columns_ref[...] = scale * pivot_scale_row * columns + jnp.where(same, 1.0, 0.0)
+            panel_ref[rows, :256] = times_t(columns_ref[:, :256], aug[:256, PANEL : PANEL + 256], HI)
+            panel_ref[rows, 256:] = times_t(columns_ref[...], aug[256:, PANEL:], HI)
 
     lane = iota((RUN, PANEL), 1).astype(f32)
     line = iota((RUN, PANEL), 0).astype(f32)
@@ -611,7 +654,15 @@
 
     for d in range(1, NY):
         picked_copy(d).wait_send()
-    spread.wait_send()
+
+    @pl.when(jnp.logical_not(stays))
+    def _():
+        away.wait_send()
+
+    @pl.when(jnp.logical_not(arrives))
+    def _():
+        onward.wait_send()
+
     for step in range(1, 5):
         for copy in c_copies(step, False):
             copy.wait_send()
@@ -645,6 +696,7 @@
             pltpu.VMEM((4, 128), jnp.int32),
             pltpu.VMEM((COLS, OWN), bf16),
             pltpu.VMEM((MINE, OWN), bf16),
+            pltpu.VMEM((COLS, OWN), bf16),
             dma((4,)),
             dma((NY,)),
             dma((NY,)),
@@ -654,8 +706,8 @@
             dma((36,)),
             dma((7,)),
             dma((7,)),
-            dma((1,)),
-            dma((1,)),
+            dma((2,)),
+            dma((2,)),
             dma((NZ,)),
             dma((NZ,)),
             dma((NY,)),

time: 112 us -> 94.2 us (0.84)
  the two profiles are of different devices: /device:TPU:38 before, /device:TPU:1 now
where the time goes in v4:
time: 94.2 us; the launch traced here: 92.6 us
  Pallas kernels  86.2 us (92%)
  local copies, waits for them, and re-layouts  5.71 us (6%)
    pallas_call x1, Pallas kernels, body(): pl.pallas_call(main_kernel, out_shape=(jax.ShapeDtypeStruct((ROWS, COLS),...  86.2 us
    unnamed x10, local copies, waits for them, and re-layouts  5.71 us

profile of v4, /device:TPU:1, one launch (start us, length us, event | category | flops | bytes accessed | tf_op | source)
XLA Modules:
  0.0 92.6 jit_solution(6619612335194692034)
XLA Ops:
  0.6 0.0 copy-start
  0.6 0.9 copy-done
  1.5 0.0 copy-start.1
  1.5 0.8 copy-done.1
  2.4 0.0 copy-start.2
  2.4 0.7 copy-done.2
  3.1 0.0 copy-start.3
  3.1 0.7 copy-done.3
  3.7 86.2 %gather_factor_panel.1 = (f32[1024,512]{1,0:T(8,128)S(1)}, f32[1024,512]{1,0:T(8,128)S(1)}) custom-call(bf16[512,128]{1,0:T(8,128)(2,1)S(1)} %copy-done, f32[1,128]{1,0:T(1,128)S(1)} %bitcast.5, f32[128,128]{1,0:T(8,128)S(1)} %bitcast.3, s32[4,128]{1,0:T(4,128)S(1)} %bitcast.4), custom_call_target="tpu_custom_call" | custom-call | tf_op jit(solution)/shard_map/gather_factor_panel/pallas_call | solution.py:677
  89.9 1.3 %copy.8 = f32[1024,512]{1,0:T(8,128)} copy(f32[1024,512]{1,0:T(8,128)S(1)} %get-tuple-element.4) | data formatting | bytes 4194304
  91.3 1.3 %copy.9 = f32[1024,512]{1,0:T(8,128)} copy(f32[1024,512]{1,0:T(8,128)S(1)} %get-tuple-element.5) | data formatting | bytes 4194304
Async XLA Ops:
  0.6 0.9 copy-start
  1.5 0.8 copy-start.1
  2.4 0.7 copy-start.2
  3.1 0.7 copy-start.3

commit v5 on v4

--- a/solution.py
+++ b/solution.py
@@ -373,6 +373,7 @@
     scaled_ref,
     picked_ref,
     mid_ref,
+    direct_ref,
     local_sem,
     qy_send,
     qy_recv,
@@ -528,9 +529,6 @@
         lax.fori_loop(0, count, step, 0)
 
     either(stays, stay.start, away.start)
-    c_pass(y).start()
-    c_advance(1)
-
     run_column = column_of((pivot_row // RUN).astype(f32))
     high_column = column_of((pivot_row // 128).astype(f32))
     low_column = column_of((pivot_row % 128).astype(f32))
@@ -543,17 +541,16 @@
 
     for d in range(1, NY):
         picked_arrival(d).wait_recv()
-    q_gather.run(0)
-    c_advance(2)
-    q_gather.run(1)
+    q_gather.run(0, 2)
     second_move()
+    c_pass(y).start()
+    c_advance(1)
     q_gather.run(2, 4)
-    c_advance(3)
     q_gather.run(4)
     either(arrives, keep.wait, onward_in.wait_recv)
     r_gather.run(0)
     q_gather.run(5, 7)
-    c_advance(4)
+    c_advance(2)
     r_gather.run(1, 3)
     q_gather.run(7, 9)
     q_gather.wait_passed()
@@ -569,14 +566,21 @@
     aug[:, :PANEL] = pivot_scale * pivot_scale_row * gram + unit
     aug[:, PANEL:] = unit
     r_gather.run(3, 7)
-    c_advance(5)
+    c_advance(3)
 
     def between(k, part):
         for block in range(4):
-
-            @pl.when(k == block)
-            def _():
-                r_gather.run(7 + 4 * block + part)
+            at = 4 * block + part
+            low, high = (7 + (19 * i) // 16 for i in (at, at + 1))
+            if low < high or at in (4, 8):
+
+                @pl.when(k == block)
+                def _():
+                    r_gather.run(low, high)
+                    if at == 4:
+                        c_advance(4)
+                    if at == 8:
+                        c_advance(5)
 
     factor_and_inverse(aug, s_ref, between)
 
@@ -616,34 +620,43 @@
                 parts.append(ref[xx, rows, pl.ds(owner, OWN)])
         return jnp.concatenate(parts, axis=1)
 
-    done = [23, 23]
-    groups = ((0, 1, 5, 2), (6, 3), (7, 4))
-    ready = {0: (21, 27, 31), 1: (20, 28, 31)}
+    done = [26, 26]
+    groups = ((0, 1, 5, 2), (6, 3, 7), (4,))
+    ready = {0: (21, 30, 31), 1: (20, 29, 31)}
+    weights = aug[:, PANEL:] * pivot_scale_row
+    everything = slice(None)
     for g, wanted in enumerate(groups):
+        if g == len(groups) - 1:
+            last_pivots = product(qp_ref, everything, wanted).astype(f32)
+            direct = jnp.dot(weights, last_pivots, precision=HI, preferred_element_type=f32)
+            for i, part in enumerate(split3(direct)):
+                direct_ref[:, i * 2 * OWN : (i + 1) * 2 * OWN] = part.astype(bf16)
         for core in range(2):
             r_gather.run_core(core, done[core], ready[core][g] + 1)
             done[core] = max(done[core], ready[core][g] + 1)
-        everything = slice(None)
-        c_part, q_part = product(c_ref, everything, wanted), product(qp_ref, everything, wanted)
+        c_part = product(c_ref, everything, wanted)
+        q_part = product(qp_ref, everything, wanted)
         for t in range(ROWS // tile):
             rows = slice(t * tile, (t + 1) * tile)
-            r_part = product(r_ref, rows, wanted)
-            gram, columns = times_t(r_part, c_part), times_t(r_part, q_part)
-            if g == 0:
-                dielectric_ref[rows, :], panel_ref[rows, :] = gram, columns
-                continue
-            gram, columns = dielectric_ref[rows, :] + gram, panel_ref[rows, :] + columns
-            if g < len(groups) - 1:
-                dielectric_ref[rows, :], panel_ref[rows, :] = gram, columns
-                continue
             scale = row_scale[rows]
             numbers = first_row + t * tile + iota((tile, COLS), 0)
+            r_part = product(r_ref, rows, wanted)
+            if g == 0:
+                dielectric_ref[rows, :], panel_ref[rows, :] = times_t(r_part, c_part), times_t(r_part, q_part)
+                continue
+            gram = dielectric_ref[rows, :] + times_t(r_part, c_part)
+            if g == 1:
+                dielectric_ref[rows, :] = gram
+                columns = panel_ref[rows, :] + times_t(r_part, q_part)
+                same = numbers == pivot_row
+                columns_ref[...] = scale * pivot_scale_row * columns + jnp.where(same, 1.0, 0.0)
+                panel_ref[rows, :256] = times_t(columns_ref[:, :256], aug[:256, PANEL : PANEL + 256], HI)
+                panel_ref[rows, 256:] = times_t(columns_ref[...], aug[256:, PANEL:], HI)
+                continue
             same = numbers == first_col + iota((tile, COLS), 1)
             dielectric_ref[rows, :] = scale * col_scale * gram + jnp.where(same, 1.0, 0.0)
-            same = numbers == pivot_row
-            columns_ref[...] = scale * pivot_scale_row * columns + jnp.where(same, 1.0, 0.0)
-            panel_ref[rows, :256] = times_t(columns_ref[:, :256], aug[:256, PANEL : PANEL + 256], HI)
-            panel_ref[rows, 256:] = times_t(columns_ref[...], aug[256:, PANEL:], HI)
+            three = jnp.concatenate([r_part] * 3, axis=1)
+            panel_ref[rows, :] = panel_ref[rows, :] + scale * times_t(three, direct_ref[...])
 
     lane = iota((RUN, PANEL), 1).astype(f32)
     line = iota((RUN, PANEL), 0).astype(f32)
@@ -697,6 +710,7 @@
             pltpu.VMEM((COLS, OWN), bf16),
             pltpu.VMEM((MINE, OWN), bf16),
             pltpu.VMEM((COLS, OWN), bf16),
+            pltpu.VMEM((PANEL, 6 * OWN), bf16),
             dma((4,)),
             dma((NY,)),
             dma((NY,)),
@@ -717,7 +731,12 @@
             collective_id=0, has_side_effects=True, vmem_limit_bytes=40 * 2**20
         ),
         name="gather_factor_panel",
-    )(pair_density, pair_weight.reshape(1, OWN), coulomb.reshape(128, 128), pivot_rows.reshape(4, 128))
+    )(
+        *(
+            pltpu.with_memory_space_constraint(a, pltpu.HBM)
+            for a in (pair_density, pair_weight.reshape(1, OWN), coulomb.reshape(128, 128), pivot_rows.reshape(4, 128))
+        )
+    )
 
 
 def solution(mesh):

time: 94.2 us -> 85.7 us (0.910); the launches traced: 92.6 us -> 85.5 us
  Pallas kernels: 86.2 us -> 82.2 us
  local copies, waits for them, and re-layouts: 5.71 us -> 2.64 us
    pallas_call x1, Pallas kernels: 86.2 us -> 82.2 us  [body(): pl.pallas_call(main_kernel, out_shape=(jax.ShapeDtypeStruct((ROWS, COLS),...]
    unnamed x10 -> x2, local copies, waits for them, and re-layouts: 5.71 us -> 2.64 us
where the time goes in v5:
time: 85.7 us; the launch traced here: 85.5 us
  Pallas kernels  82.2 us (96%)
  local copies, waits for them, and re-layouts  2.64 us (3%)
    pallas_call x1, Pallas kernels, body(): pl.pallas_call(main_kernel, out_shape=(jax.ShapeDtypeStruct((ROWS, COLS),...  82.2 us
    unnamed x2, local copies, waits for them, and re-layouts  2.64 us

profile of v5, /device:TPU:1, one launch (start us, length us, event | category | flops | bytes accessed | tf_op | source)
XLA Modules:
  0.0 85.5 jit_solution(4472694434890794753)
XLA Ops:
  0.6 82.2 %gather_factor_panel.1 = (f32[1024,512]{1,0:T(8,128)S(1)}, f32[1024,512]{1,0:T(8,128)S(1)}) custom-call(bf16[512,128]{1,0:T(8,128)(2,1)} %density_in.1, f32[1,128]{1,0:T(1,128)} %bitcast.5, f32[128,128]{1,0:T(8,128)} %bitcast.3, s32[4,128]{1,0:T(4,128)} %bitcast.4), custom_call_target="tpu_custom_call" | custom-call | tf_op jit(solution)/shard_map/gather_factor_panel/pallas_call | solution.py:690
  82.9 1.3 %copy.8 = f32[1024,512]{1,0:T(8,128)} copy(f32[1024,512]{1,0:T(8,128)S(1)} %get-tuple-element.4) | data formatting | bytes 4194304
  84.2 1.3 %copy.9 = f32[1024,512]{1,0:T(8,128)} copy(f32[1024,512]{1,0:T(8,128)S(1)} %get-tuple-element.5) | data formatting | bytes 4194304

commit v6 on v5

--- a/solution.py
+++ b/solution.py
@@ -192,12 +192,12 @@
             def _():
                 self.process(self.events(core)[first:last])
 
-    def drain(self):
+    def drain(self, first=0, last=None):
         for core in range(2):
 
             @pl.when(self.place[1] == core)
             def _():
-                for waits, sends, passes in self.events(core):
+                for waits, sends, passes in self.events(core)[first:last]:
                     for ref, k, device in sends:
                         self.copy(ref, k, device).wait_send()
                     for line in passes:
@@ -429,10 +429,11 @@
     r_gather = RowGather(r_slot, (rg_send, rg_recv), place)
 
     barrier = pltpu.get_barrier_semaphore()
-    greeted = [(lax.rem(y + d, NY), c, x, z) for d in range(1, NY)]
+    greeted = [middle, origin]
+    greeted += [(lax.rem(y + d, NY), c, x, z) for d in (4, 3, 5, 2, 6, 1, 7)]
     greeted += [(y, c, x, lax.rem(z + d, NZ)) for d in range(1, NZ)]
     greeted += [(y, c, lax.rem(x + d, NX), z) for d in range(1, NX)]
-    greeted += [partner, middle, origin]
+    greeted += [partner]
     for device in greeted:
         pl.semaphore_signal(barrier, 1, device_id=device, device_id_type=MESH_ID)
 
@@ -546,9 +547,9 @@
     c_pass(y).start()
     c_advance(1)
     q_gather.run(2, 4)
-    q_gather.run(4)
     either(arrives, keep.wait, onward_in.wait_recv)
     r_gather.run(0)
+    q_gather.run(4)
     q_gather.run(5, 7)
     c_advance(2)
     r_gather.run(1, 3)
@@ -619,6 +620,24 @@
                 owner = pl.multiple_of(owner_of(xx, zz) * OWN, OWN)
                 parts.append(ref[xx, rows, pl.ds(owner, OWN)])
         return jnp.concatenate(parts, axis=1)
+
+    for d in range(1, NY):
+        picked_copy(d).wait_send()
+
+    @pl.when(jnp.logical_not(stays))
+    def _():
+        away.wait_send()
+
+    @pl.when(jnp.logical_not(arrives))
+    def _():
+        onward.wait_send()
+
+    for step in range(1, 5):
+        for copy in c_copies(step, False):
+            copy.wait_send()
+    repeat(NY, lambda i: c_pass(i).wait_send())
+    q_gather.drain()
+    r_gather.drain(0, 20)
 
     done = [26, 26]
     groups = ((0, 1, 5, 2), (6, 3, 7), (4,))
@@ -665,23 +684,7 @@
         over = (line == within[q : q + 1]) & (lane >= position[q : q + 1])
         panel_ref[rows, :] = jnp.where(over, jnp.broadcast_to(top[q : q + 1, :], (RUN, PANEL)), panel_ref[rows, :])
 
-    for d in range(1, NY):
-        picked_copy(d).wait_send()
-
-    @pl.when(jnp.logical_not(stays))
-    def _():
-        away.wait_send()
-
-    @pl.when(jnp.logical_not(arrives))
-    def _():
-        onward.wait_send()
-
-    for step in range(1, 5):
-        for copy in c_copies(step, False):
-            copy.wait_send()
-    repeat(NY, lambda i: c_pass(i).wait_send())
-    q_gather.drain()
-    r_gather.drain()
+    r_gather.drain(20)
 
 
 def body(pair_density, pair_weight, coulomb, pivot_rows):

time: 85.7 us -> 86.1 us (level)
  no operation moved by 1% of the time
where the time goes in v6:
time: 86.1 us; the launch traced here: 85.9 us
  Pallas kernels  82.6 us (96%)
  local copies, waits for them, and re-layouts  2.64 us (3%)
    pallas_call x1, Pallas kernels, body(): pl.pallas_call(main_kernel, out_shape=(jax.ShapeDtypeStruct((ROWS, COLS),...  82.6 us
    unnamed x2, local copies, waits for them, and re-layouts  2.64 us

profile of v6, /device:TPU:1, one launch (start us, length us, event | category | flops | bytes accessed | tf_op | source)
XLA Modules:
  0.0 85.9 jit_solution(7262437021538436985)
XLA Ops:
  0.6 82.6 %gather_factor_panel.1 = (f32[1024,512]{1,0:T(8,128)S(1)}, f32[1024,512]{1,0:T(8,128)S(1)}) custom-call(bf16[512,128]{1,0:T(8,128)(2,1)} %density_in.1, f32[1,128]{1,0:T(1,128)} %bitcast.5, f32[128,128]{1,0:T(8,128)} %bitcast.3, s32[4,128]{1,0:T(4,128)} %bitcast.4), custom_call_target="tpu_custom_call" | custom-call | tf_op jit(solution)/shard_map/gather_factor_panel/pallas_call | solution.py:693
  83.3 1.3 %copy.8 = f32[1024,512]{1,0:T(8,128)} copy(f32[1024,512]{1,0:T(8,128)S(1)} %get-tuple-element.4) | data formatting | bytes 4194304
  84.6 1.3 %copy.9 = f32[1024,512]{1,0:T(8,128)} copy(f32[1024,512]{1,0:T(8,128)S(1)} %get-tuple-element.5) | data formatting | bytes 4194304
